TPU v7x, 32 devices: a whole 2x2x4 slice. The times are simulated.
32 devices in a mesh: batch: 2 (over x), ctx: 4 (over y, core), mp: 4 (over z).
Axes of the slice: x: 2, y: 2, z: 4, core: 2. Of those that a mesh axis runs over, the one named last changes fastest.
Arguments:
- hidden_in: bfloat16 [4, 512, 1024], P('batch', 'ctx'), may hold values from -6 to 6
- segment_ids: int32 [4, 512], P('batch', 'ctx'), may hold values from 0 to 3, never falling along the last dimension, each value on 1 to 256 neighbouring positions
- gains: bfloat16 [2, 2, 1024], P(None, None, ('batch', 'ctx', 'mp')), may hold values from 0.5 to 1.5
- biases: bfloat16 [2, 10, 1024], P(None, None, ('batch', 'ctx', 'mp')), may hold values from -3 to 3
- w_qkv: bfloat16 [2, 1024, 3, 1024], P(None, ('batch', 'ctx'), None, 'mp'), may hold values from -0.1875 to 0.1875
- w_out_t: bfloat16 [2, 1024, 1024], P(None, ('batch', 'ctx'), 'mp'), may hold values from -0.5 to 0.5
- w_up: bfloat16 [2, 1024, 4096], P(None, ('batch', 'ctx'), 'mp'), may hold values from -0.1875 to 0.1875
- w_down_t: bfloat16 [2, 1024, 4096], P(None, ('batch', 'ctx'), 'mp'), may hold values from -0.09375 to 0.09375
- grad_out: bfloat16 [4, 512, 1024], P('batch', 'ctx'), may hold values from -6 to 6
Outputs:
- output: bfloat16 [4, 512, 1024], P('batch', 'ctx')
- grad_in: bfloat16 [4, 512, 1024], P('batch', 'ctx')
- grad_gains: float32 [2, 2, 1024], P(None, None, ('batch', 'ctx', 'mp'))
- grad_biases: float32 [2, 10, 1024], P(None, None, ('batch', 'ctx', 'mp'))
- grad_qkv: float32 [2, 1024, 3, 1024], P(None, ('batch', 'ctx'), None, 'mp')
- grad_attn_out: float32 [2, 1024, 1024], P(None, ('batch', 'ctx'), 'mp')
- grad_up: float32 [2, 1024, 4096], P(None, ('batch', 'ctx'), 'mp')
- grad_down: float32 [2, 1024, 4096], P(None, ('batch', 'ctx'), 'mp')
Inputs may be any that keep to these rules, and one draw needn't show every extreme that they name: `segment_ids`: document numbers never fall along a sequence; every document spans 1 to 256 tokens, and one of each sequence spans exactly that many.
All inputs are finite; a program needn't handle non-finite values.
Results may differ from a plain program's by a relative error of at most 0.023.
Values may be sent and summed in bfloat16 or wider, within the bound.
A program may use at most 128 MiB of HBM per device.

v0:
```python
import math

import jax
import jax.numpy as jnp
from jax import lax
from jax.sharding import PartitionSpec as P

HEADS = 16
HEAD = 64


EPS = 1e-05
GELU_C = 0.7978845608028654
GELU_K = 0.044715


def norm_parts(values):
    center = values - jnp.mean(values, -1, keepdims=True)
    inverse = lax.rsqrt(jnp.mean(center * center, -1, keepdims=True) + EPS)
    return (center * inverse, inverse)


def norm_back(grad_y, normed, inverse, gain):
    scaled = grad_y * gain
    return inverse * (
        scaled
        - jnp.mean(scaled, -1, keepdims=True)
        - normed * jnp.mean(scaled * normed, -1, keepdims=True)
    )


def gelu_parts(values):
    bend = jnp.tanh(GELU_C * (values + GELU_K * values * values * values))
    return (0.5 * values * (1.0 + bend), bend)


def gelu_slope(values, bend):
    return 0.5 * (1.0 + bend) + 0.5 * values * (1.0 - bend * bend) * GELU_C * (
        1.0 + 3.0 * GELU_K * values * values
    )


def block_mask(q_pos, q_seg, key_seg, start, block):
    k_pos = start + jnp.arange(block, dtype=jnp.int32)
    seg_keys = lax.dynamic_slice_in_dim(key_seg, start, block, 1)
    mask = (k_pos[None, None, :] <= q_pos[None, :, None]) & (
        seg_keys[:, None, :] == q_seg[:, :, None]
    )
    return mask[:, None]


def block_scores(query, keys, q_pos, start, block, slope, scale):
    k_pos = start + jnp.arange(block, dtype=jnp.int32)
    dist = (q_pos[:, None] - k_pos[None, :]).astype(jnp.float32)
    score = jnp.einsum("sqhd,skhd->shqk", query, keys, preferred_element_type=jnp.float32)
    return score * scale - slope[None, :, None, None] * dist[None, None]


def attend_forward(query, kv_all, q_pos, q_seg, key_seg, slope):
    seqs, rows, heads, width = query.shape
    length = kv_all.shape[1]
    block = min(512, length)
    scale = 1.0 / math.sqrt(width)

    def step(carry, index):
        start = index * block
        mask = block_mask(q_pos, q_seg, key_seg, start, block)

        def work(state):
            acc, total = state
            pair = lax.dynamic_slice_in_dim(kv_all, start, block, 1).reshape(
                seqs, block, 2, heads, width
            )
            score = block_scores(query, pair[:, :, 0], q_pos, start, block, slope, scale)
            expo = jnp.where(mask, jnp.exp(jnp.where(mask, score, 0.0)), 0.0)
            acc = acc + jnp.einsum(
                "shqk,skhd->sqhd",
                expo.astype(jnp.bfloat16),
                pair[:, :, 1],
                preferred_element_type=jnp.float32,
            )
            return (acc, total + jnp.sum(expo, -1))

        return (lax.cond(jnp.any(mask), work, lambda state: state, carry), None)

    init = (jnp.zeros(query.shape, jnp.float32), jnp.zeros((seqs, heads, rows), jnp.float32))
    (acc, total), _ = lax.scan(step, init, jnp.arange(length // block, dtype=jnp.int32))
    ctx = (acc / jnp.transpose(total, (0, 2, 1))[..., None]).astype(jnp.bfloat16)
    return (ctx, jnp.log(total))


def attend_backward(query, kv_all, q_pos, q_seg, key_seg, slope, ctx, lse, dctx):
    seqs, rows, heads, width = query.shape
    length = kv_all.shape[1]
    block = min(512, length)
    scale = 1.0 / math.sqrt(width)
    delta = jnp.transpose(
        jnp.sum(dctx.astype(jnp.float32) * ctx.astype(jnp.float32), -1), (0, 2, 1)
    )

    def step(carry, index):
        start = index * block
        mask = block_mask(q_pos, q_seg, key_seg, start, block)

        def work(state):
            grad_q, grad_kv = state
            pair = lax.dynamic_slice_in_dim(kv_all, start, block, 1).reshape(
                seqs, block, 2, heads, width
            )
            score = block_scores(query, pair[:, :, 0], q_pos, start, block, slope, scale)
            prob = jnp.where(mask, jnp.exp(jnp.where(mask, score - lse[..., None], 0.0)), 0.0)
            grad_v = jnp.einsum(
                "shqk,sqhd->skhd",
                prob.astype(jnp.bfloat16),
                dctx,
                preferred_element_type=jnp.float32,
            )
            grad_p = jnp.einsum(
                "sqhd,skhd->shqk", dctx, pair[:, :, 1], preferred_element_type=jnp.float32
            )
            grad_s = (prob * (grad_p - delta[..., None])).astype(jnp.bfloat16)
            grad_q = (
                grad_q
                + jnp.einsum(
                    "shqk,skhd->sqhd", grad_s, pair[:, :, 0], preferred_element_type=jnp.float32
                )
                * scale
            )
            grad_k = (
                jnp.einsum("shqk,sqhd->skhd", grad_s, query, preferred_element_type=jnp.float32)
                * scale
            )
            piece = jnp.stack([grad_k, grad_v], 2).reshape(seqs, block, 2, heads * width)
            return (grad_q, lax.dynamic_update_slice_in_dim(grad_kv, piece, start, 1))

        return (lax.cond(jnp.any(mask), work, lambda state: state, carry), None)

    init = (
        jnp.zeros(query.shape, jnp.float32),
        jnp.zeros((seqs, length, 2, heads * width), jnp.float32),
    )
    (grad_q, grad_kv), _ = lax.scan(step, init, jnp.arange(length // block, dtype=jnp.int32))
    return (grad_q, grad_kv)


def per_device(hidden_in, segment_ids, gains, biases, w_qkv, w_out_t, w_up, w_down_t, grad_out):
    seqs, rows, width = hidden_in.shape
    layers = w_qkv.shape[0]
    cols = w_qkv.shape[3]
    ff_cols = w_up.shape[2]
    heads = cols // HEAD
    mp_count = lax.axis_size("mp")
    mp_index = lax.axis_index("mp")
    all_gains, all_biases = (
        lax.all_gather(gains, ("batch", "ctx", "mp"), axis=2, tiled=True),
        lax.all_gather(biases, ("batch", "ctx", "mp"), axis=2, tiled=True),
    )
    key_seg = lax.all_gather(segment_ids, "ctx", axis=1, tiled=True)
    q_pos = lax.axis_index("ctx") * rows + jnp.arange(rows, dtype=jnp.int32)
    head_ids = (mp_index * heads + jnp.arange(heads, dtype=jnp.int32)).astype(jnp.float32)
    slope = jnp.exp2(-8.0 * (head_ids + 1.0) / HEADS)
    own = (jnp.arange(width, dtype=jnp.int32) // cols == mp_index).astype(jnp.float32)
    full_ff = ff_cols * mp_count

    def place(values, offset, total):
        return lax.dynamic_update_slice_in_dim(jnp.zeros((total,), jnp.float32), values, offset, 0)

    def unpack(layer):
        vec = all_biases[layer]
        query_bias = lax.dynamic_slice_in_dim(vec[2], mp_index * cols, cols, 0)
        value_bias = lax.dynamic_slice_in_dim(vec[3], mp_index * cols, cols, 0)
        up_projection_bias = lax.dynamic_slice_in_dim(
            vec[6:].reshape(-1), mp_index * ff_cols, ff_cols, 0
        )
        return (vec, query_bias, value_bias, up_projection_bias)

    def forward_layer(layer, state, weights):
        query_weight, w_o, up_weight, w_d = weights
        vec, query_bias, value_bias, up_projection_bias = unpack(layer)
        normed1, _ = norm_parts(state)
        first_activation = (normed1 * all_gains[layer, 0] + vec[0]).astype(jnp.bfloat16)
        query_key_value = jnp.einsum(
            "bph,hue->bpue", first_activation, query_weight, preferred_element_type=jnp.float32
        )
        shift = jnp.stack([query_bias, jnp.zeros_like(query_bias), value_bias])
        qkv_bf = (query_key_value + shift).astype(jnp.bfloat16)
        kv_all = lax.all_gather(qkv_bf[:, :, 1:], "ctx", axis=1, tiled=True)
        query = qkv_bf[:, :, 0].reshape(seqs, rows, heads, HEAD)
        ctx, lse = attend_forward(query, kv_all, q_pos, segment_ids, key_seg, slope)
        ctx_flat = ctx.reshape(seqs, rows, cols)
        part = jnp.einsum("slc,oc->slo", ctx_flat, w_o, preferred_element_type=jnp.float32)
        mid = state + lax.psum(part, "mp") + vec[4]
        normed2, _ = norm_parts(mid)
        second_activation = (normed2 * all_gains[layer, 1] + vec[1]).astype(jnp.bfloat16)
        up_projected = (
            jnp.einsum(
                "nhz,zb->nhb", second_activation, up_weight, preferred_element_type=jnp.float32
            )
            + up_projection_bias
        )
        act, _ = gelu_parts(up_projected)
        act_bf = act.astype(jnp.bfloat16)
        down = jnp.einsum("slf,of->slo", act_bf, w_d, preferred_element_type=jnp.float32)
        result = mid + lax.psum(down, "mp") + vec[5]
        return (
            result,
            (
                state,
                first_activation,
                qkv_bf,
                kv_all,
                ctx_flat,
                lse,
                mid,
                second_activation,
                up_projected,
                act_bf,
            ),
        )

    state = hidden_in.astype(jnp.float32)
    saves = []
    for layer in range(layers):
        weights = (
            lax.all_gather(w_qkv[layer], ("batch", "ctx"), axis=0, tiled=True),
            lax.all_gather(w_out_t[layer], ("batch", "ctx"), axis=0, tiled=True),
            lax.all_gather(w_up[layer], ("batch", "ctx"), axis=0, tiled=True),
            lax.all_gather(w_down_t[layer], ("batch", "ctx"), axis=0, tiled=True),
        )
        state, saved = forward_layer(layer, state, weights)
        saves.append((weights, saved))
    output = state.astype(jnp.bfloat16)
    grad = grad_out.astype(jnp.float32)
    gain_rows = [None] * layers
    bias_rows = [None] * layers
    matrix_grads = [None] * layers
    for layer in reversed(range(layers)):
        kept_weights, saved = saves[layer]
        (
            x_in,
            first_activation,
            qkv_bf,
            kv_kept,
            ctx_flat,
            lse,
            mid,
            second_activation,
            up_projected,
            act_bf,
        ) = saved
        query_weight, w_o, up_weight, w_d = (
            lax.all_gather(w_qkv[layer], ("batch", "ctx"), axis=0, tiled=True),
            lax.all_gather(w_out_t[layer], ("batch", "ctx"), axis=0, tiled=True),
            lax.all_gather(w_up[layer], ("batch", "ctx"), axis=0, tiled=True),
            lax.all_gather(w_down_t[layer], ("batch", "ctx"), axis=0, tiled=True),
        )
        kv_all = lax.all_gather(qkv_bf[:, :, 1:], "ctx", axis=1, tiled=True)
        gain1 = all_gains[layer, 0]
        gain2 = all_gains[layer, 1]
        grad_bf = grad.astype(jnp.bfloat16)
        grad_bd = jnp.sum(grad, (0, 1))
        grad_wd = jnp.einsum("slo,slf->of", grad_bf, act_bf, preferred_element_type=jnp.float32)
        dact = jnp.einsum("slo,of->slf", grad_bf, w_d, preferred_element_type=jnp.float32)
        _, bend = gelu_parts(up_projected)
        dup = dact * gelu_slope(up_projected, bend)
        grad_bu = jnp.sum(dup, (0, 1))
        up_gradient_half_precision = dup.astype(jnp.bfloat16)
        up_weight_gradient = jnp.einsum(
            "qwi,qwn->in",
            second_activation,
            up_gradient_half_precision,
            preferred_element_type=jnp.float32,
        )
        da2 = lax.psum(
            jnp.einsum(
                "cju,xu->cjx",
                up_gradient_half_precision,
                up_weight,
                preferred_element_type=jnp.float32,
            ),
            "mp",
        )
        normed2, inverse2 = norm_parts(mid)
        grad_g2 = jnp.sum(da2 * normed2, (0, 1))
        grad_b2 = jnp.sum(da2, (0, 1))
        gx2 = grad + norm_back(da2, normed2, inverse2, gain2)
        grad_bo = jnp.sum(gx2, (0, 1))
        gx2_bf = gx2.astype(jnp.bfloat16)
        grad_wo = jnp.einsum("slo,slc->oc", gx2_bf, ctx_flat, preferred_element_type=jnp.float32)
        dctx = jnp.einsum("slo,oc->slc", gx2_bf, w_o, preferred_element_type=jnp.float32).astype(
            jnp.bfloat16
        )
        query = qkv_bf[:, :, 0].reshape(seqs, rows, heads, HEAD)
        ctx_heads = ctx_flat.reshape(seqs, rows, heads, HEAD)
        dctx_heads = dctx.reshape(seqs, rows, heads, HEAD)
        grad_q, grad_kv_terms = attend_backward(
            query, kv_all, q_pos, segment_ids, key_seg, slope, ctx_heads, lse, dctx_heads
        )
        grad_kv = lax.psum_scatter(grad_kv_terms, "ctx", scatter_dimension=1, tiled=True)
        grad_qf = grad_q.reshape(seqs, rows, cols)
        grad_bq = jnp.sum(grad_qf, (0, 1))
        value_bias_gradient = jnp.sum(grad_kv[:, :, 1], (0, 1))
        packed_projection_gradient = jnp.concatenate([grad_qf[:, :, None], grad_kv], 2).astype(
            jnp.bfloat16
        )
        query_weight_gradient = jnp.einsum(
            "ebz,ebpy->zpy",
            first_activation,
            packed_projection_gradient,
            preferred_element_type=jnp.float32,
        )
        da1 = lax.psum(
            jnp.einsum(
                "aewu,vwu->aev",
                packed_projection_gradient,
                query_weight,
                preferred_element_type=jnp.float32,
            ),
            "mp",
        )
        normed1, inverse1 = norm_parts(x_in)
        grad_g1 = jnp.sum(da1 * normed1, (0, 1))
        grad_b1 = jnp.sum(da1, (0, 1))
        grad = gx2 + norm_back(da1, normed1, inverse1, gain1)
        gain_rows[layer] = jnp.stack([grad_g1 * own, grad_g2 * own])
        head_rows = jnp.stack(
            [
                grad_b1 * own,
                grad_b2 * own,
                place(grad_bq, mp_index * cols, width),
                place(value_bias_gradient, mp_index * cols, width),
                grad_bo * own,
                grad_bd * own,
            ]
        )
        unit_rows = place(grad_bu, mp_index * ff_cols, full_ff).reshape(full_ff // width, width)
        bias_rows[layer] = jnp.concatenate([head_rows, unit_rows], 0)
        matrix_grads[layer] = (
            lax.psum_scatter(
                query_weight_gradient.astype(jnp.bfloat16),
                ("batch", "ctx"),
                scatter_dimension=0,
                tiled=True,
            ).astype(jnp.float32),
            lax.psum_scatter(
                grad_wo.astype(jnp.bfloat16), ("batch", "ctx"), scatter_dimension=0, tiled=True
            ).astype(jnp.float32),
            lax.psum_scatter(
                up_weight_gradient.astype(jnp.bfloat16),
                ("batch", "ctx"),
                scatter_dimension=0,
                tiled=True,
            ).astype(jnp.float32),
            lax.psum_scatter(
                grad_wd.astype(jnp.bfloat16), ("batch", "ctx"), scatter_dimension=0, tiled=True
            ).astype(jnp.float32),
        )
    grad_gains, grad_biases = (
        lax.psum_scatter(
            jnp.stack(gain_rows), ("batch", "ctx", "mp"), scatter_dimension=2, tiled=True
        ),
        lax.psum_scatter(
            jnp.stack(bias_rows), ("batch", "ctx", "mp"), scatter_dimension=2, tiled=True
        ),
    )
    grad_qkv = jnp.stack([item[0] for item in matrix_grads])
    grad_attn_out = jnp.stack([item[1] for item in matrix_grads])
    grad_up = jnp.stack([item[2] for item in matrix_grads])
    grad_down = jnp.stack([item[3] for item in matrix_grads])
    return (
        output,
        grad.astype(jnp.bfloat16),
        grad_gains,
        grad_biases,
        grad_qkv,
        grad_attn_out,
        grad_up,
        grad_down,
    )


def solution(mesh):
    in_specs = (
        P("batch", "ctx", None),
        P("batch", "ctx"),
        P(None, None, ("batch", "ctx", "mp")),
        P(None, None, ("batch", "ctx", "mp")),
        P(None, ("batch", "ctx"), None, "mp"),
        P(None, ("batch", "ctx"), "mp"),
        P(None, ("batch", "ctx"), "mp"),
        P(None, ("batch", "ctx"), "mp"),
        P("batch", "ctx", None),
    )
    out_specs = (
        P("batch", "ctx", None),
        P("batch", "ctx", None),
        P(None, None, ("batch", "ctx", "mp")),
        P(None, None, ("batch", "ctx", "mp")),
        P(None, ("batch", "ctx"), None, "mp"),
        P(None, ("batch", "ctx"), "mp"),
        P(None, ("batch", "ctx"), "mp"),
        P(None, ("batch", "ctx"), "mp"),
    )
    return jax.shard_map(
        per_device, mesh=mesh, in_specs=in_specs, out_specs=out_specs, check_vma=False
    )
```

profile of v0, /device:TPU:0, one launch (start us, length us, event | category | flops | bytes accessed | tf_op | source)
XLA Modules:
  0.0 1558.4 jit_solution(14924374231961429402)
XLA Ops:
  10.7 74.2 %all_gather.51 = bf16[2,10,1024]{1,0,2:T(2,128)(2,1)S(1)} all-gather(bf16[2,10,32]{1,0,2:T(2,128)(2,1)S(1)} %copy.109), channel_id=1, replica_groups=mesh['batch'=2,'ctx'=4,'mp'=4] {'batch','ctx','mp'}, dimensions={2}, use_global_device_ids=true | all-gather | bytes 42240 | tf_op jit(solution)/shard_map/all_gather | solution.py:156
  84.8 2.5 fusion.155
  89.5 68.0 %all_gather.50 = bf16[2,2,1024]{1,0,2:T(2,128)(2,1)S(1)} all-gather(bf16[2,2,32]{1,0,2:T(2,128)(2,1)S(1)} %copy.108), channel_id=1, replica_groups=mesh['batch'=2,'ctx'=4,'mp'=4] {'batch','ctx','mp'}, dimensions={2}, use_global_device_ids=true | all-gather | bytes 8448 | tf_op jit(solution)/shard_map/all_gather | solution.py:155
  158.0 18.2 %fusion.103 = (f32[1024]{0:T(1024)S(1)}, f32[1024]{0:T(1024)S(1)}, f32[1024]{0:T(1024)S(1)}, f32[1024]{0:T(1024)S(1)}) fusion(bf16[2,2,1024]{1,0,2:T(2,128)(2,1)S(1)} %all_gather.50), kind=kLoop, calls=%fused_computation.161 | loop fusion | flops 4096 | bytes 24576 | tf_op jit(solution)/shard_map/mul | solution.py:194
  176.3 24.9 %fusion.101 = (f32[1024]{0:T(1024)}, f32[1024]{0:T(1024)}, f32[1024]{0:T(1024)}, f32[1024]{0:T(1024)S(1)}, f32[1024]{0:T(1024)S(1)}, /*index=5*/f32[1024]{0:T(1024)S(1)}, f32[1024]{0:T(1024)S(1)}, f32[1024]{0:T(1024)S(1)}) fusion(bf16[2,10,1024]{1,0,2:T(2,128)(2,1)S(1)} %all_gather.51), kind=kLoop, calls=%fused_computation.157 | loop fusion | flops 8192 | bytes 49152 | tf_op jit(solution)/shard_map/add | solution.py:204
  204.1 5.1 all_gather.49
  213.1 9.1 all-gather.1
  223.0 6.8 conditional.4
  226.9 2.5 fusion.148
  235.7 45.8 %all-reduce.9.cloned.1.call-done = f32[2,128,1024]{2,1,0:T(8,128)} async-done(((f32[2,128,1024]{2,1,0:T(8,128)}), f32[2,128,1024]{2,1,0:T(8,128)}) %all-reduce.9.cloned.1.call-update) | async-done | bytes 1048592 | tf_op jit(solution)/shard_map/psum | solution.py:192
  283.3 27.7 %all-gather.23.cloned.1.call-done = bf16[1,1024,1024]{2,1,0:T(8,128)(2,1)} async-done(((bf16[1,128,1024]{2,1,0:T(8,128)(2,1)}), bf16[1,1024,1024]{2,1,0:T(8,128)(2,1)}) %all-gather.23.cloned.1.call-update) | async-done | bytes 2097168 | tf_op jit(solution)/shard_map/all_gather | solution.py:227
  310.9 2.4 fusion.47
  313.3 27.7 %all-gather.25.cloned.1.call-done = bf16[1,1024,1024]{2,1,0:T(8,128)(2,1)} async-done(((bf16[1,128,1024]{2,1,0:T(8,128)(2,1)}), bf16[1,1024,1024]{2,1,0:T(8,128)(2,1)}) %all-gather.25.cloned.1.call-update) | async-done | bytes 2097168 | tf_op jit(solution)/shard_map/all_gather | solution.py:228
  341.0 3.4 fusion.26
  345.3 51.3 %all-reduce.11.cloned.1.call-done = f32[2,128,1024]{2,1,0:T(8,128)} async-done(((f32[2,128,1024]{2,1,0:T(8,128)}), f32[2,128,1024]{2,1,0:T(8,128)}) %all-reduce.11.cloned.1.call-update) | async-done | bytes 1048592 | tf_op jit(solution)/shard_map/psum | solution.py:204
  398.2 25.1 %all-gather.27.cloned.1.call-done = bf16[1,1024,3,256]{3,1,2,0:T(8,128)(2,1)} async-done(((bf16[1,128,3,256]{3,1,2,0:T(8,128)(2,1)}), bf16[1,1024,3,256]{3,1,2,0:T(8,128)(2,1)}) %all-gather.27.cloned.1.call-update) | async-done | bytes 1572880 | tf_op jit(solution)/shard_map/all_gather | solution.py:225
  426.2 9.8 all-gather.5
  436.8 6.2 all-gather.19.cloned.1.call-done
  443.0 7.7 conditional.5
  447.7 2.5 fusion.149
  454.7 49.4 %all-reduce.13.cloned.1.call-done = f32[2,128,1024]{2,1,0:T(8,128)} async-done(((f32[2,128,1024]{2,1,0:T(8,128)}), f32[2,128,1024]{2,1,0:T(8,128)}) %all-reduce.13.cloned.1.call-update) | async-done | bytes 1048592 | tf_op jit(solution)/shard_map/psum | solution.py:192
  505.9 27.1 %all-gather.29.cloned.1.call-done = bf16[1,1024,1024]{2,1,0:T(8,128)(2,1)} async-done(((bf16[1,128,1024]{2,1,0:T(8,128)(2,1)}), bf16[1,1024,1024]{2,1,0:T(8,128)(2,1)}) %all-gather.29.cloned.1.call-update) | async-done | bytes 2097168 | tf_op jit(solution)/shard_map/all_gather | solution.py:227
  533.0 3.4 fusion.53
  536.3 26.9 %all-gather.31.cloned.1.call-done = bf16[1,1024,1024]{2,1,0:T(8,128)(2,1)} async-done(((bf16[1,128,1024]{2,1,0:T(8,128)(2,1)}), bf16[1,1024,1024]{2,1,0:T(8,128)(2,1)}) %all-gather.31.cloned.1.call-update) | async-done | bytes 2097168 | tf_op jit(solution)/shard_map/all_gather | solution.py:228
  563.3 3.9 fusion.158
  572.0 49.8 %all-reduce.15.cloned.1.call-done = f32[2,128,1024]{2,1,0:T(8,128)} async-done(((f32[2,128,1024]{2,1,0:T(8,128)}), f32[2,128,1024]{2,1,0:T(8,128)}) %all-reduce.15.cloned.1.call-update) | async-done | bytes 1048592 | tf_op jit(solution)/shard_map/psum | solution.py:274
  621.8 2.4 multiply_reduce_fusion
  629.9 16.3 %conditional.6 = (f32[2,512,2,256]{1,3,0,2:T(8,128)}, f32[1,256]{1,0:T(1,128)}, bf16[2,128,1,256]{3,1,2,0:T(8,128)(2,1)S(1)}) conditional(s32[]{:T(128)} %convert_element_type.234, (f32[2,512,2,256]{1,3,0,2:T(8,128)}, f32[2,128,4,64]{1,3,2,0:T(8,128)S(1)}) %tuple.89, (pred[2,1,128,512]{3,2,0,1:T(8,128)(4,1)}, ...), branch_computations={%region_23.24_spmd.clone, %region_24.25_spmd.clone} | conditional | flops 341704448 | bytes 28077692 | solution.py:136
  634.8 2.4 exponential_select_fusion.3
  642.5 3.1 pad_maximum_fusion.1
  646.2 3.0 copy.120
  649.3 30.6 %reduce-scatter.17.cloned.1.call-done = f32[2,128,2,256]{3,1,2,0:T(8,128)} async-done(((f32[2,512,2,256]{3,1,2,0:T(8,128)}), f32[2,128,2,256]{3,1,2,0:T(8,128)}) %reduce-scatter.17.cloned.1.call-update) | async-done | bytes 524304 | tf_op jit(solution)/shard_map/reduce_scatter | solution.py:299
  681.7 3.0 fusion.44
  684.7 52.0 %all-reduce.17.cloned.1.call-done = f32[2,128,1024]{2,1,0:T(8,128)} async-done(((f32[2,128,1024]{2,1,0:T(8,128)}), f32[2,128,1024]{2,1,0:T(8,128)}) %all-reduce.17.cloned.1.call-update) | async-done | bytes 1048592 | tf_op jit(solution)/shard_map/psum | solution.py:312
  736.7 2.5 multiply_reduce_fusion.1
  746.1 50.7 %all-reduce.19.cloned.1.call-done = f32[2,128,1024]{2,1,0:T(8,128)} async-done(((f32[2,128,1024]{2,1,0:T(8,128)}), f32[2,128,1024]{2,1,0:T(8,128)}) %all-reduce.19.cloned.1.call-update) | async-done | bytes 1048592 | tf_op jit(solution)/shard_map/psum | solution.py:274
  796.8 2.4 multiply_reduce_fusion.2
  804.8 15.0 conditional.7
  807.2 2.4 copy.123
  809.6 2.3 exponential_select_fusion.2
  816.7 3.1 pad_maximum_fusion
  819.9 2.9 copy.124
  822.9 3.7 fusion.18
  826.6 26.8 %reduce-scatter.19.cloned.1.call-done = f32[2,128,2,256]{3,1,2,0:T(8,128)} async-done(((f32[2,512,2,256]{3,1,2,0:T(8,128)}), f32[2,128,2,256]{3,1,2,0:T(8,128)}) %reduce-scatter.19.cloned.1.call-update) | async-done | bytes 524304 | tf_op jit(solution)/shard_map/reduce_scatter | solution.py:299
  855.2 3.0 fusion.41
  858.6 2.4 fusion.60
  861.1 2.4 fusion.59
  863.6 3.3 bitcast_convert_fusion.2
  867.0 3.2 bitcast_convert_fusion.3
  871.3 3.4 fusion.32
  876.0 3.4 bitcast_convert_fusion.1
  882.3 62.3 %all-reduce.21.cloned.1.call-done = (f32[2,128,1024]{2,1,0:T(8,128)}, f32[2,128,1024]{2,1,0:T(8,128)}) async-done(((f32[2,128,1024]{2,1,0:T(8,128)}, f32[2,128,1024]{2,1,0:T(8,128)}), (f32[2,128,1024]{2,1,0:T(8,128)}, f32[2,128,1024]{2,1,0:T(8,128)})) %all-reduce.21.cloned.1.call-update) | async-done | bytes 2097168 | tf_op jit(solution)/shard_map/psum | solution.py:204
  947.7 2.6 reshape.647
  951.9 2.7 reshape.649
  958.8 22.5 %reduce-scatter.27.cloned.1.call-done = bf16[128,256]{1,0:T(8,128)(2,1)} async-done(((bf16[1024,256]{1,0:T(8,128)(2,1)}), bf16[128,256]{1,0:T(8,128)(2,1)}) %reduce-scatter.27.cloned.1.call-update) | async-done | bytes 65552 | tf_op jit(solution)/shard_map/reduce_scatter | solution.py:345
  981.3 37.8 %reduce-scatter.25.cloned.1.call-done = bf16[128,256]{1,0:T(8,128)(2,1)} async-done(((bf16[1024,256]{1,0:T(8,128)(2,1)}), bf16[128,256]{1,0:T(8,128)(2,1)}) %reduce-scatter.25.cloned.1.call-update) | async-done | bytes 65552 | tf_op jit(solution)/shard_map/reduce_scatter | solution.py:345
  1020.7 42.7 %reduce-scatter.31.cloned.1.call-done = bf16[128,1024]{1,0:T(8,128)(2,1)} async-done(((bf16[1024,1024]{1,0:T(8,128)(2,1)}), bf16[128,1024]{1,0:T(8,128)(2,1)}) %reduce-scatter.31.cloned.1.call-update) | async-done | bytes 262160 | tf_op jit(solution)/shard_map/reduce_scatter | solution.py:348
  1063.4 44.4 %reduce-scatter.29.cloned.1.call-done = bf16[128,1024]{1,0:T(8,128)(2,1)} async-done(((bf16[1024,1024]{1,0:T(8,128)(2,1)}), bf16[128,1024]{1,0:T(8,128)(2,1)}) %reduce-scatter.29.cloned.1.call-update) | async-done | bytes 262160 | tf_op jit(solution)/shard_map/reduce_scatter | solution.py:348
  1109.9 42.4 %reduce-scatter.35.cloned.1.call-done = bf16[128,1024]{1,0:T(8,128)(2,1)} async-done(((bf16[1024,1024]{1,0:T(8,128)(2,1)}), bf16[128,1024]{1,0:T(8,128)(2,1)}) %reduce-scatter.35.cloned.1.call-update) | async-done | bytes 262160 | tf_op jit(solution)/shard_map/reduce_scatter | solution.py:354
  1152.2 44.4 %reduce-scatter.33.cloned.1.call-done = bf16[128,1024]{1,0:T(8,128)(2,1)} async-done(((bf16[1024,1024]{1,0:T(8,128)(2,1)}), bf16[128,1024]{1,0:T(8,128)(2,1)}) %reduce-scatter.33.cloned.1.call-update) | async-done | bytes 262160 | tf_op jit(solution)/shard_map/reduce_scatter | solution.py:354
  1201.1 134.4 %reduce-scatter.37.cloned.1.call-done = f32[32,4]{1,0:T(8,128)} async-done(((f32[1024,4]{1,0:T(8,128)}), f32[32,4]{1,0:T(8,128)}) %reduce-scatter.37.cloned.1.call-update) | async-done | bytes 528
  1337.0 133.0 %reduce-scatter.39.cloned.1.call-done = f32[32,20]{1,0:T(8,128)} async-done(((f32[1024,20]{1,0:T(8,128)}), f32[32,20]{1,0:T(8,128)}) %reduce-scatter.39.cloned.1.call-update) | async-done | bytes 2576
  1471.6 36.1 %reduce-scatter.23.cloned.1.call-done = bf16[128,3,256]{2,0,1:T(8,128)(2,1)} async-done(((bf16[1024,3,256]{2,0,1:T(8,128)(2,1)}), bf16[128,3,256]{2,0,1:T(8,128)(2,1)}) %reduce-scatter.23.cloned.1.call-update) | async-done | bytes 196624 | tf_op jit(solution)/shard_map/reduce_scatter | solution.py:339
  1507.7 41.5 %reduce-scatter.21.cloned.1.call-done = bf16[128,3,256]{2,0,1:T(8,128)(2,1)} async-done(((bf16[1024,3,256]{2,0,1:T(8,128)(2,1)}), bf16[128,3,256]{2,0,1:T(8,128)(2,1)}) %reduce-scatter.21.cloned.1.call-update) | async-done | bytes 196624 | tf_op jit(solution)/shard_map/reduce_scatter | solution.py:339
  (422 shorter events, 113.5 us)
Async XLA Ops:
  7.2 194.0 %all-gather.21.cloned.1.call-start = ((), (), s32[]{:S(2)}) async-start(), calls=%async_computation.30 | async-start | bytes 1769472 | tf_op jit(solution)/shard_map/all_gather | solution.py:225
  9.0 214.0 %all-gather.17.cloned.1.call-start = ((), (), s32[]{:S(2)}) async-start(), calls=%async_computation.12 | async-start | bytes 1310720 | tf_op jit(solution)/shard_map/all_gather | solution.py:187
  84.8 72.7 %copy-start.4 = (bf16[2,128,1024]{2,1,0:T(8,128)(2,1)S(1)}, bf16[2,128,1024]{2,1,0:T(8,128)(2,1)}, u32[]{:S(2)}) copy-start(bf16[2,128,1024]{2,1,0:T(8,128)(2,1)} %param.17) | copy-start | bytes 1572868
  157.7 43.5 %copy-start.63 = (f32[2,128]{1,0:T(2,128)}, f32[2,128]{1,0:T(2,128)S(1)}, u32[]{:S(2)}) copy-start(f32[2,128]{1,0:T(2,128)S(1)} %broadcast_multiply_fusion.15) | copy-start | bytes 3076
  158.0 43.2 %copy-start.89 = (f32[2,128]{1,0:T(2,128)}, f32[2,128]{1,0:T(2,128)S(1)}, u32[]{:S(2)}) copy-start(f32[2,128]{1,0:T(2,128)S(1)} %add_rsqrt_fusion.3) | copy-start | bytes 3076
  176.2 24.9 %copy-start.52 = (f32[1024]{0:T(1024)}, f32[1024]{0:T(1024)S(1)}, u32[]{:S(2)}) copy-start(f32[1024]{0:T(1024)S(1)} %get-tuple-element.615) | copy-start | bytes 12292
  176.2 247.0 %copy-start.54 = (f32[1024]{0:T(1024)}, f32[1024]{0:T(1024)S(1)}, u32[]{:S(2)}) copy-start(f32[1024]{0:T(1024)S(1)} %get-tuple-element.613) | copy-start | bytes 12292
  201.2 109.8 %copy-start.84 = (f32[1024]{0:T(1024)}, f32[1024]{0:T(1024)S(1)}, u32[]{:S(2)}) copy-start(f32[1024]{0:T(1024)S(1)} %get-tuple-element.609) | copy-start | bytes 12292
  201.2 222.1 %copy-start.102 = (f32[1024]{0:T(1024)}, f32[1024]{0:T(1024)S(1)}, u32[]{:S(2)}) copy-start(f32[1024]{0:T(1024)S(1)} %get-tuple-element.607) | copy-start | bytes 12292
  201.2 11.9 copy-start.49
  204.1 77.5 %all-reduce.9.cloned.1.call-start = ((), (), s32[]{:S(2)}) async-start(), calls=%async_computation.13 | async-start | bytes 2097152 | tf_op jit(solution)/shard_map/psum | solution.py:192
  222.2 7.7 copy-start.9
  231.3 79.6 %all-gather.23.cloned.1.call-start = ((), (), s32[]{:S(2)}) async-start(), calls=%async_computation.31 | async-start | bytes 2359296 | tf_op jit(solution)/shard_map/all_gather | solution.py:227
  232.2 108.8 %all-gather.25.cloned.1.call-start = ((), (), s32[]{:S(2)}) async-start(), calls=%async_computation.32 | async-start | bytes 2359296 | tf_op jit(solution)/shard_map/all_gather | solution.py:228
  233.1 163.4 %all-reduce.11.cloned.1.call-start = ((), (), s32[]{:S(2)}) async-start(), calls=%async_computation.14 | async-start | bytes 2097152 | tf_op jit(solution)/shard_map/psum | solution.py:204
  283.0 30.3 %copy-start.56 = (f32[2,128]{1,0:T(2,128)}, f32[2,128]{1,0:T(2,128)S(1)}, u32[]{:S(2)}) copy-start(f32[2,128]{1,0:T(2,128)S(1)} %broadcast_multiply_fusion.14) | copy-start | bytes 3076
  283.3 30.1 %copy-start.65 = (f32[2,128]{1,0:T(2,128)}, f32[2,128]{1,0:T(2,128)S(1)}, u32[]{:S(2)}) copy-start(f32[2,128]{1,0:T(2,128)S(1)} %add_rsqrt_fusion.2) | copy-start | bytes 3076
  313.3 31.1 %copy-start.38 = (f32[2,128,1024]{2,1,0:T(8,128)}, f32[2,128,1024]{2,1,0:T(8,128)S(1)}, u32[]{:S(2)}) copy-start(f32[2,128,1024]{2,1,0:T(8,128)S(1)} %fusion.47) | copy-start | bytes 3145732
  344.5 78.8 %all-gather.27.cloned.1.call-start = ((), (), s32[]{:S(2)}) async-start(), calls=%async_computation.33 | async-start | bytes 1769472 | tf_op jit(solution)/shard_map/all_gather | solution.py:225
  345.2 97.7 %all-gather.19.cloned.1.call-start = ((), (), s32[]{:S(2)}) async-start(), calls=%async_computation.15 | async-start | bytes 1310720 | tf_op jit(solution)/shard_map/all_gather | solution.py:187
  397.9 27.4 %copy-start.80 = (f32[2,128]{1,0:T(2,128)}, f32[2,128]{1,0:T(2,128)S(1)}, u32[]{:S(2)}) copy-start(f32[2,128]{1,0:T(2,128)S(1)} %broadcast_multiply_fusion.13) | copy-start | bytes 3076
  398.2 27.9 %copy-start.91 = (f32[2,128]{1,0:T(2,128)}, f32[2,128]{1,0:T(2,128)S(1)}, u32[]{:S(2)}) copy-start(f32[2,128]{1,0:T(2,128)S(1)} %add_rsqrt_fusion.1) | copy-start | bytes 3076
  426.1 78.1 %all-reduce.13.cloned.1.call-start = ((), (), s32[]{:S(2)}) async-start(), calls=%async_computation.16 | async-start | bytes 2097152 | tf_op jit(solution)/shard_map/psum | solution.py:192
  436.0 14.8 copy-start.11
  443.0 4.8 copy-start.51
  450.7 53.5 %copy-start.88 = (f32[1024]{0:T(1024)S(1)}, f32[1024]{0:T(1024)}, u32[]{:S(2)}) copy-start(f32[1024]{0:T(1024)} %get-tuple-element.606) | copy-start | bytes 12292
  450.7 53.4 %copy-start.31 = (bf16[2,128,4,64]{1,3,2,0:T(8,128)(2,1)}, bf16[2,128,4,64]{1,3,2,0:T(8,128)(2,1)S(1)}, u32[]{:S(2)}) copy-start(bf16[2,128,4,64]{1,3,2,0:T(8,128)(2,1)S(1)} %divide_convert_fusion) | copy-start | bytes 393220
  452.1 80.9 %all-gather.29.cloned.1.call-start = ((), (), s32[]{:S(2)}) async-start(), calls=%async_computation.34 | async-start | bytes 2359296 | tf_op jit(solution)/shard_map/all_gather | solution.py:227
  452.7 110.6 %all-gather.31.cloned.1.call-start = ((), (), s32[]{:S(2)}) async-start(), calls=%async_computation.35 | async-start | bytes 2359296 | tf_op jit(solution)/shard_map/all_gather | solution.py:228
  453.4 168.3 %all-reduce.15.cloned.1.call-start = ((), (), s32[]{:S(2)}) async-start(), calls=%async_computation.17 | async-start | bytes 2097152 | tf_op jit(solution)/shard_map/psum | solution.py:274
  504.2 28.8 %copy-start.86 = (f32[1024]{0:T(1024)S(1)}, f32[1024]{0:T(1024)}, u32[]{:S(2)}) copy-start(f32[1024]{0:T(1024)} %get-tuple-element.605) | copy-start | bytes 12292
  505.6 118.6 %copy-start.59 = (f32[2,128]{1,0:T(2,128)}, f32[2,128]{1,0:T(2,128)S(1)}, u32[]{:S(2)}) copy-start(f32[2,128]{1,0:T(2,128)S(1)} %broadcast_multiply_fusion.12) | copy-start | bytes 3076
  505.9 118.3 %copy-start.68 = (f32[2,128]{1,0:T(2,128)}, f32[2,128]{1,0:T(2,128)S(1)}, u32[]{:S(2)}) copy-start(f32[2,128]{1,0:T(2,128)S(1)} %add_rsqrt_fusion) | copy-start | bytes 3076
  569.7 110.1 %reduce-scatter.17.cloned.1.call-start = ((), (), s32[]{:S(2)}) async-start(), calls=%async_computation.18 | async-start | bytes 2621440 | tf_op jit(solution)/shard_map/reduce_scatter | solution.py:299
  646.2 34.7 %copy-start.43 = (bf16[2,128,1,256]{3,1,2,0:T(8,128)(2,1)}, bf16[2,128,1,256]{3,1,2,0:T(8,128)(2,1)S(1)}, u32[]{:S(2)}) copy-start(bf16[2,128,1,256]{3,1,2,0:T(8,128)(2,1)S(1)} %get-tuple-element.586) | copy-start | bytes 393220
  649.3 87.4 %all-reduce.17.cloned.1.call-start = ((), (), s32[]{:S(2)}) async-start(), calls=%async_computation.19 | async-start | bytes 2097152 | tf_op jit(solution)/shard_map/psum | solution.py:312
  681.0 55.7 %copy-start.55 = (f32[1024]{0:T(1024)S(1)}, f32[1024]{0:T(1024)}, u32[]{:S(2)}) copy-start(f32[1024]{0:T(1024)} %copy-done.54) | copy-start | bytes 12292
  684.6 54.5 %copy-start.81 = (f32[2,128]{1,0:T(2,128)S(1)}, f32[2,128]{1,0:T(2,128)}, u32[]{:S(2)}) copy-start(f32[2,128]{1,0:T(2,128)} %copy-done.80) | copy-start | bytes 3076
  684.6 54.5 %copy-start.92 = (f32[2,128]{1,0:T(2,128)S(1)}, f32[2,128]{1,0:T(2,128)}, u32[]{:S(2)}) copy-start(f32[2,128]{1,0:T(2,128)} %copy-done.91) | copy-start | bytes 3076
  684.7 112.1 %all-reduce.19.cloned.1.call-start = ((), (), s32[]{:S(2)}) async-start(), calls=%async_computation.20 | async-start | bytes 2097152 | tf_op jit(solution)/shard_map/psum | solution.py:274
  743.7 53.1 %copy-start.57 = (f32[2,128]{1,0:T(2,128)S(1)}, f32[2,128]{1,0:T(2,128)}, u32[]{:S(2)}) copy-start(f32[2,128]{1,0:T(2,128)} %copy-done.56) | copy-start | bytes 3076
  743.7 53.1 %copy-start.66 = (f32[2,128]{1,0:T(2,128)S(1)}, f32[2,128]{1,0:T(2,128)}, u32[]{:S(2)}) copy-start(f32[2,128]{1,0:T(2,128)} %copy-done.65) | copy-start | bytes 3076
  745.5 108.0 %reduce-scatter.19.cloned.1.call-start = ((), (), s32[]{:S(2)}) async-start(), calls=%async_computation.21 | async-start | bytes 2621440 | tf_op jit(solution)/shard_map/reduce_scatter | solution.py:299
  819.9 34.7 %copy-start.45 = (bf16[2,128,1,256]{3,1,2,0:T(8,128)(2,1)}, bf16[2,128,1,256]{3,1,2,0:T(8,128)(2,1)S(1)}, u32[]{:S(2)}) copy-start(bf16[2,128,1,256]{3,1,2,0:T(8,128)(2,1)S(1)} %get-tuple-element.587) | copy-start | bytes 393220
  822.8 121.8 %all-reduce.21.cloned.1.call-start = ((), (), s32[]{:S(2)}) async-start(), calls=%async_computation.38 | async-start | bytes 4194304 | tf_op jit(solution)/shard_map/psum | solution.py:204
  858.3 5.3 copy-start.60
  858.3 5.3 copy-start.69
  858.3 5.3 copy-start.87
  858.3 123.0 %reduce-scatter.27.cloned.1.call-start = ((), (), s32[]{:S(2)}) async-start(), calls=%async_computation.25 | async-start | bytes 589824 | tf_op jit(solution)/shard_map/reduce_scatter | solution.py:345
  861.0 158.1 %reduce-scatter.25.cloned.1.call-start = ((), (), s32[]{:S(2)}) async-start(), calls=%async_computation.24 | async-start | bytes 589824 | tf_op jit(solution)/shard_map/reduce_scatter | solution.py:345
  863.5 199.8 %reduce-scatter.31.cloned.1.call-start = ((), (), s32[]{:S(2)}) async-start(), calls=%async_computation.27 | async-start | bytes 2359296 | tf_op jit(solution)/shard_map/reduce_scatter | solution.py:348
  866.9 240.9 %reduce-scatter.29.cloned.1.call-start = ((), (), s32[]{:S(2)}) async-start(), calls=%async_computation.26 | async-start | bytes 2359296 | tf_op jit(solution)/shard_map/reduce_scatter | solution.py:348
  870.3 282.0 %reduce-scatter.35.cloned.1.call-start = ((), (), s32[]{:S(2)}) async-start(), calls=%async_computation.29 | async-start | bytes 2359296 | tf_op jit(solution)/shard_map/reduce_scatter | solution.py:354
  874.8 321.9 %reduce-scatter.33.cloned.1.call-start = ((), (), s32[]{:S(2)}) async-start(), calls=%async_computation.28 | async-start | bytes 2359296 | tf_op jit(solution)/shard_map/reduce_scatter | solution.py:354
  879.5 65.1 %copy-start.5 = (bf16[2,128,1024]{2,1,0:T(8,128)(2,1)S(1)}, bf16[2,128,1024]{2,1,0:T(8,128)(2,1)}, u32[]{:S(2)}) copy-start(bf16[2,128,1024]{2,1,0:T(8,128)(2,1)} %param.17) | copy-start | bytes 1572868
  879.5 65.1 %copy-start.53 = (f32[1024]{0:T(1024)S(1)}, f32[1024]{0:T(1024)}, u32[]{:S(2)}) copy-start(f32[1024]{0:T(1024)} %copy-done.52) | copy-start | bytes 12292
  879.5 65.1 %copy-start.64 = (f32[2,128]{1,0:T(2,128)S(1)}, f32[2,128]{1,0:T(2,128)}, u32[]{:S(2)}) copy-start(f32[2,128]{1,0:T(2,128)} %copy-done.63) | copy-start | bytes 3076
  879.5 65.1 %copy-start.90 = (f32[2,128]{1,0:T(2,128)S(1)}, f32[2,128]{1,0:T(2,128)}, u32[]{:S(2)}) copy-start(f32[2,128]{1,0:T(2,128)} %copy-done.89) | copy-start | bytes 3076
  879.5 456.0 %reduce-scatter.37.cloned.1.call-start = ((), (), s32[]{:S(2)}) async-start(), calls=%async_computation.36 | async-start | bytes 540672
  950.4 519.7 %reduce-scatter.39.cloned.1.call-start = ((), (), s32[]{:S(2)}) async-start(), calls=%async_computation.37 | async-start | bytes 540672
  954.7 553.0 %reduce-scatter.23.cloned.1.call-start = ((), (), s32[]{:S(2)}) async-start(), calls=%async_computation.23 | async-start | bytes 1769472 | tf_op jit(solution)/shard_map/reduce_scatter | solution.py:339
  956.8 592.4 %reduce-scatter.21.cloned.1.call-start = ((), (), s32[]{:S(2)}) async-start(), calls=%async_computation.22 | async-start | bytes 1769472 | tf_op jit(solution)/shard_map/reduce_scatter | solution.py:339
  958.8 240.1 %copy-start.33 = (f32[2,128,1024]{2,1,0:T(8,128)S(1)}, f32[2,128,1024]{2,1,0:T(8,128)}, u32[]{:S(2)}) copy-start(f32[2,128,1024]{2,1,0:T(8,128)} %get-tuple-element.616) | copy-start | bytes 3145732
  958.8 240.1 %copy-start.83 = (f32[1024]{0:T(1024)S(1)}, f32[1024]{0:T(1024)}, u32[]{:S(2)}) copy-start(f32[1024]{0:T(1024)} %get-tuple-element.604) | copy-start | bytes 12292
  (68 other events, 156.5 us)
Sparse Core Ops, SparseCore 0:
  10.5 28.6 all-gather.20
  204.2 14.2 all-gather.16
  231.4 50.0 all-reduce.8
  283.9 27.0 all-gather.22
  313.2 27.7 all-gather.24
  344.6 51.8 all-reduce.10
  398.4 24.8 all-gather.26
  426.2 16.6 all-gather.18
  452.2 51.8 all-reduce.12
  505.9 27.0 all-gather.28
  535.4 27.7 all-gather.30
  569.8 51.8 all-reduce.14
  649.4 30.4 reduce-scatter.16
  684.8 51.8 all-reduce.16
  745.6 51.1 all-reduce.18
  823.0 30.4 reduce-scatter.18
  858.4 86.1 all-reduce.20
  948.1 33.1 reduce-scatter.26
  985.0 34.0 reduce-scatter.24
  1022.2 41.0 reduce-scatter.30
  1066.6 41.1 reduce-scatter.28
  1111.1 41.1 reduce-scatter.34
  1155.5 41.1 reduce-scatter.32
  1199.3 136.1 reduce-scatter.36
  1337.8 132.2 reduce-scatter.38
  1473.2 34.3 reduce-scatter.22
  1510.8 38.3 reduce-scatter.20
where the time goes:
time: 1570 us; the launch traced here: 1560 us
  waiting for transfers between devices  1140 us (73%)
  blocking collectives  166 us (11%)
  other arithmetic  96.6 us (6%)
  matrix products  78.5 us (5%)
  local copies, waits for them, and re-layouts  57.6 us (4%)
  between operations  16.8 us (1%)
    unnamed x29, waiting for transfers between devices  270 us
    psum x2, waiting for transfers between devices, forward_layer(): result = mid + lax.psum(down, 'mp') + vec[5]  114 us
    psum x2, waiting for transfers between devices, per_device(): lax.psum(jnp.einsum('cju,xu->cjx', up_gradient_half_precision, up_weight,...  100 us
    psum x2, waiting for transfers between devices, forward_layer(): mid = state + lax.psum(part, 'mp') + vec[4]  95.2 us
    reduce_scatter x2, waiting for transfers between devices, per_device(): lax.psum_scatter(up_weight_gradient.astype(jnp.bfloat16), ('batch', 'ctx'...  87.1 us
    reduce_scatter x2, waiting for transfers between devices, per_device(): lax.psum_scatter(grad_wd.astype(jnp.bfloat16), ('batch', 'ctx'), scatter_...  86.8 us
    reduce_scatter x2, waiting for transfers between devices, per_device(): lax.psum_scatter(query_weight_gradient.astype(jnp.bfloat16), ('batch', 'c...  77.6 us
    all_gather x1, blocking collectives, per_device(): lax.all_gather(biases, ('batch', 'ctx', 'mp'), axis=2, tiled=True)  74.2 us
  transfers between devices with their start and end apart: 27, of which 25 were waited for; matrix products, arithmetic and copies ran while one was open for 8% of the time, Pallas kernels for 0%

commit v1 on v0

--- a/solution.py
+++ b/solution.py
@@ -3,6 +3,8 @@
 import jax
 import jax.numpy as jnp
 from jax import lax
+from jax.experimental import pallas as pl
+from jax.experimental.pallas import tpu as pltpu
 from jax.sharding import PartitionSpec as P
 
 HEADS = 16
@@ -38,6 +40,252 @@
     return 0.5 * (1.0 + bend) + 0.5 * values * (1.0 - bend * bend) * GELU_C * (
         1.0 + 3.0 * GELU_K * values * values
     )
+
+
+MESH = pl.DeviceIdType.MESH
+ANY = pl.BlockSpec(memory_space=pl.ANY)
+VMEM = pl.BlockSpec(memory_space=pltpu.VMEM)
+
+
+def rank_of(kind):
+    if kind in ("mp", "ctx"):
+        return lax.axis_index(kind), lax.axis_size(kind)
+    count = lax.axis_size("ctx")
+    if kind == "core":
+        return lax.rem(lax.axis_index("ctx"), 2), 2
+    flat = lax.axis_index("batch") * count + lax.axis_index("ctx")
+    if kind == "chip":
+        return flat // 2, lax.axis_size("batch") * count // 2
+    return flat, lax.axis_size("batch") * count
+
+
+def device_of(kind, rank):
+    if kind in ("mp", "ctx"):
+        return {kind: rank}
+    count = lax.axis_size("ctx")
+    if kind == "core":
+        return {"ctx": (lax.axis_index("ctx") // 2) * 2 + rank}
+    flat = rank * 2 + lax.rem(lax.axis_index("ctx"), 2)
+    return {"batch": flat // count, "ctx": lax.rem(flat, count)}
+
+
+def greet(devices):
+    barrier = pltpu.get_barrier_semaphore()
+    for device in devices:
+        pl.semaphore_signal(barrier, inc=1, device_id=device, device_id_type=MESH)
+    pl.semaphore_wait(barrier, len(devices))
+
+
+def remote(src, dst, send, recv, device):
+    return pltpu.make_async_remote_copy(
+        src_ref=src, dst_ref=dst, send_sem=send, recv_sem=recv,
+        device_id=device, device_id_type=MESH,
+    )
+
+
+def total_mp(values, name):
+    rows, width = values.shape
+    count = lax.axis_size("mp")
+    piece = rows // count
+
+    def kernel(x_ref, o_ref, held, send, recv):
+        me, _ = rank_of("mp")
+        ranks = [lax.rem(me + t, count) for t in range(1, count)]
+        devices = [device_of("mp", rank) for rank in ranks]
+        greet(devices)
+        mine = pl.ds(pl.multiple_of(me * piece, piece), piece)
+        first = []
+        for t in range(count - 1):
+            theirs = pl.ds(pl.multiple_of(ranks[t] * piece, piece), piece)
+            copy = remote(x_ref.at[theirs], held.at[t], send.at[0, t], recv.at[0, t], devices[t])
+            copy.start()
+            first.append(copy)
+        acc = x_ref[mine, :].astype(jnp.float32)
+        for t in range(count - 1):
+            first[t].wait_recv()
+            acc = acc + held[t].astype(jnp.float32)
+        o_ref[mine, :] = acc.astype(jnp.bfloat16)
+        second = []
+        for t in range(count - 1):
+            copy = remote(o_ref.at[mine], o_ref.at[mine], send.at[1, t], recv.at[1, t], devices[t])
+            copy.start()
+            second.append(copy)
+        for copy in first:
+            copy.wait_send()
+        for copy in second:
+            copy.wait_send()
+        for t in range(count - 1):
+            source = lax.rem(me + count - 1 - t, count)
+            theirs = pl.ds(pl.multiple_of(source * piece, piece), piece)
+            remote(
+                o_ref.at[theirs], o_ref.at[theirs], send.at[1, t], recv.at[1, t], devices[t]
+            ).wait_recv()
+
+    return pl.pallas_call(
+        kernel,
+        out_shape=jax.ShapeDtypeStruct((rows, width), jnp.bfloat16),
+        in_specs=[VMEM],
+        out_specs=VMEM,
+        scratch_shapes=[
+            pltpu.VMEM((count - 1, piece, width), jnp.bfloat16),
+            pltpu.SemaphoreType.DMA((2, count - 1)),
+            pltpu.SemaphoreType.DMA((2, count - 1)),
+        ],
+        compiler_params=pltpu.CompilerParams(collective_id=0, has_side_effects=True),
+        name="total_mp",
+    )(values)
+
+
+def spread(arrays, kind, ident):
+    me, count = rank_of(kind)
+    size = len(arrays)
+
+    def kernel(*refs):
+        ins, outs, (send, recv) = refs[:size], refs[size : 2 * size], refs[2 * size :]
+        rank, _ = rank_of(kind)
+        devices = [device_of(kind, lax.rem(rank + t, count)) for t in range(1, count)]
+        greet(devices)
+        copies = []
+        for t in range(count - 1):
+            for i in range(size):
+                copy = remote(ins[i], outs[i].at[rank], send.at[i, t], recv.at[i, t], devices[t])
+                copy.start()
+                copies.append(copy)
+        for copy in copies:
+            copy.wait_send()
+        for t in range(count - 1):
+            source = lax.rem(rank + count - 1 - t, count)
+            for i in range(size):
+                remote(
+                    ins[i], outs[i].at[source], send.at[i, t], recv.at[i, t], devices[t]
+                ).wait_recv()
+
+    outs = pl.pallas_call(
+        kernel,
+        out_shape=[jax.ShapeDtypeStruct((count,) + a.shape, a.dtype) for a in arrays],
+        in_specs=[ANY] * size,
+        out_specs=[ANY] * size,
+        scratch_shapes=[pltpu.SemaphoreType.DMA((size, count - 1))] * 2,
+        compiler_params=pltpu.CompilerParams(collective_id=ident, has_side_effects=True),
+        name="spread_" + kind,
+    )(*arrays)
+    return [lax.dynamic_update_index_in_dim(o, a, me, 0) for o, a in zip(outs, arrays)]
+
+
+def spread_all(arrays, ident):
+    me, total = rank_of("flat")
+    size = len(arrays)
+    chips = total // 2
+
+    def kernel(*refs):
+        ins, outs, (send, recv, send2, recv2) = refs[:size], refs[size : 2 * size], refs[2 * size :]
+        chip, _ = rank_of("chip")
+        core, _ = rank_of("core")
+        rank = chip * 2 + core
+        other = chip * 2 + 1 - core
+        devices = [device_of("chip", lax.rem(chip + t, chips)) for t in range(1, chips)]
+        sibling = device_of("core", 1 - core)
+        greet(devices + [sibling])
+        sent = []
+        for i in range(size):
+            for t in range(chips - 1):
+                copy = remote(ins[i], outs[i].at[rank], send.at[i, t], recv.at[i, t], devices[t])
+                copy.start()
+                sent.append(copy)
+        for i in range(size):
+            copy = remote(
+                ins[i], outs[i].at[rank], send2.at[i, 0], recv2.at[i, 0], sibling
+            )
+            copy.start()
+            sent.append(copy)
+        for i in range(size):
+            for t in range(chips - 1):
+                source = lax.rem(chip + chips - 1 - t, chips) * 2 + core
+                remote(
+                    ins[i], outs[i].at[source], send.at[i, t], recv.at[i, t], devices[t]
+                ).wait_recv()
+                copy = remote(
+                    outs[i].at[source], outs[i].at[source],
+                    send2.at[i, t + 1], recv2.at[i, t + 1], sibling,
+                )
+                copy.start()
+                sent.append(copy)
+        for copy in sent:
+            copy.wait_send()
+        for i in range(size):
+            remote(
+                ins[i], outs[i].at[other], send2.at[i, 0], recv2.at[i, 0], sibling
+            ).wait_recv()
+            for t in range(chips - 1):
+                source = lax.rem(chip + chips - 1 - t, chips) * 2 + 1 - core
+                remote(
+                    ins[i], outs[i].at[source],
+                    send2.at[i, t + 1], recv2.at[i, t + 1], sibling,
+                ).wait_recv()
+
+    outs = pl.pallas_call(
+        kernel,
+        out_shape=[jax.ShapeDtypeStruct((total,) + a.shape, a.dtype) for a in arrays],
+        in_specs=[ANY] * size,
+        out_specs=[ANY] * size,
+        scratch_shapes=[pltpu.SemaphoreType.DMA((size, chips - 1))] * 2
+        + [pltpu.SemaphoreType.DMA((size, chips))] * 2,
+        compiler_params=pltpu.CompilerParams(collective_id=ident, has_side_effects=True),
+        name="spread_all",
+    )(*arrays)
+    return [lax.dynamic_update_index_in_dim(o, a, me, 0) for o, a in zip(outs, arrays)]
+
+
+def trade(arrays, kind, ident, dim=0):
+    me, count = rank_of(kind)
+    size = len(arrays)
+
+    def pick(ref, rank):
+        return ref.at[rank] if dim == 0 else ref.at[:, rank]
+
+    def kernel(*refs):
+        ins, outs, (send, recv) = refs[:size], refs[size : 2 * size], refs[2 * size :]
+        rank, _ = rank_of(kind)
+        ranks = [lax.rem(rank + t, count) for t in range(1, count)]
+        devices = [device_of(kind, peer) for peer in ranks]
+        greet(devices)
+        copies = []
+        for t in range(count - 1):
+            for i in range(size):
+                copy = remote(
+                    pick(ins[i], ranks[t]), outs[i].at[t], send.at[i, t], recv.at[i, t], devices[t]
+                )
+                copy.start()
+                copies.append(copy)
+        for copy in copies:
+            copy.wait()
+
+    def shape_of(a):
+        return (count - 1,) + a.shape[:dim] + a.shape[dim + 1 :]
+
+    outs = pl.pallas_call(
+        kernel,
+        out_shape=[jax.ShapeDtypeStruct(shape_of(a), a.dtype) for a in arrays],
+        in_specs=[ANY] * size,
+        out_specs=[ANY] * size,
+        scratch_shapes=[pltpu.SemaphoreType.DMA((size, count - 1))] * 2,
+        compiler_params=pltpu.CompilerParams(collective_id=ident, has_side_effects=True),
+        name="trade_" + kind,
+    )(*arrays)
+    sums = []
+    for got, a in zip(outs, arrays):
+        acc = lax.dynamic_index_in_dim(a, me, dim, keepdims=False).astype(jnp.float32)
+        for t in range(count - 1):
+            acc = acc + got[t].astype(jnp.float32)
+        sums.append(acc)
+    return sums
+
+
+def scatter_all(arrays, ident):
+    _, total = rank_of("flat")
+    split = [a.reshape((total // 2, 2, a.shape[0] // total) + a.shape[1:]) for a in arrays]
+    halves = trade(split, "core", ident, dim=1)
+    return trade([h.astype(a.dtype) for h, a in zip(halves, arrays)], "chip", ident + 1)
 
 
 def block_mask(q_pos, q_seg, key_seg, start, block):
@@ -81,10 +329,15 @@
             )
             return (acc, total + jnp.sum(expo, -1))
 
+        if length == block:
+            return (work(carry), None)
         return (lax.cond(jnp.any(mask), work, lambda state: state, carry), None)
 
     init = (jnp.zeros(query.shape, jnp.float32), jnp.zeros((seqs, heads, rows), jnp.float32))
-    (acc, total), _ = lax.scan(step, init, jnp.arange(length // block, dtype=jnp.int32))
+    if length == block:
+        (acc, total), _ = step(init, 0)
+    else:
+        (acc, total), _ = lax.scan(step, init, jnp.arange(length // block, dtype=jnp.int32))
     ctx = (acc / jnp.transpose(total, (0, 2, 1))[..., None]).astype(jnp.bfloat16)
     return (ctx, jnp.log(total))
 
@@ -131,15 +384,22 @@
                 * scale
             )
             piece = jnp.stack([grad_k, grad_v], 2).reshape(seqs, block, 2, heads * width)
+            if length == block:
+                return (grad_q, piece)
             return (grad_q, lax.dynamic_update_slice_in_dim(grad_kv, piece, start, 1))
 
+        if length == block:
+            return (work(carry), None)
         return (lax.cond(jnp.any(mask), work, lambda state: state, carry), None)
 
     init = (
         jnp.zeros(query.shape, jnp.float32),
         jnp.zeros((seqs, length, 2, heads * width), jnp.float32),
     )
-    (grad_q, grad_kv), _ = lax.scan(step, init, jnp.arange(length // block, dtype=jnp.int32))
+    if length == block:
+        (grad_q, grad_kv), _ = step(init, 0)
+    else:
+        (grad_q, grad_kv), _ = lax.scan(step, init, jnp.arange(length // block, dtype=jnp.int32))
     return (grad_q, grad_kv)
 
 
@@ -151,11 +411,46 @@
     heads = cols // HEAD
     mp_count = lax.axis_size("mp")
     mp_index = lax.axis_index("mp")
-    all_gains, all_biases = (
-        lax.all_gather(gains, ("batch", "ctx", "mp"), axis=2, tiled=True),
-        lax.all_gather(biases, ("batch", "ctx", "mp"), axis=2, tiled=True),
-    )
-    key_seg = lax.all_gather(segment_ids, "ctx", axis=1, tiled=True)
+    layers_rows = gains.shape[0] * gains.shape[1]
+    bias_count = biases.shape[0] * biases.shape[1]
+    part = gains.shape[2]
+    vectors = jnp.concatenate(
+        [gains.reshape(layers_rows, part), biases.reshape(bias_count, part)], 0
+    )
+    (vectors,) = spread([vectors], "mp", 1)
+    first = spread_all(
+        [
+            w_qkv[0].reshape(-1, 3 * cols),
+            w_out_t[0],
+            w_up[0],
+            w_down_t[0],
+            vectors.reshape(-1, part),
+            segment_ids,
+        ],
+        2,
+    )
+    owners = first[4].shape[0]
+    vectors = jnp.transpose(
+        first[4].reshape(owners, mp_count, layers_rows + bias_count, part), (2, 0, 1, 3)
+    ).reshape(layers_rows + bias_count, width)
+    all_gains = vectors[:layers_rows].reshape(gains.shape[:2] + (width,))
+    all_biases = vectors[layers_rows:].reshape(biases.shape[:2] + (width,))
+    ctx_count = lax.axis_size("ctx")
+    key_seg = lax.dynamic_slice_in_dim(
+        first[5], lax.axis_index("batch") * ctx_count, ctx_count, 0
+    )
+    key_seg = jnp.transpose(key_seg, (1, 0, 2)).reshape(seqs, ctx_count * rows)
+    first_weights = (
+        first[0].reshape(width, 3, cols),
+        first[1].reshape(width, cols),
+        first[2].reshape(width, ff_cols),
+        first[3].reshape(width, ff_cols),
+    )
+
+    def sum_mp(values):
+        flat = values.reshape(seqs * rows, width).astype(jnp.bfloat16)
+        return total_mp(flat, "mp").reshape(values.shape).astype(jnp.float32)
+
     q_pos = lax.axis_index("ctx") * rows + jnp.arange(rows, dtype=jnp.int32)
     head_ids = (mp_index * heads + jnp.arange(heads, dtype=jnp.int32)).astype(jnp.float32)
     slope = jnp.exp2(-8.0 * (head_ids + 1.0) / HEADS)
@@ -184,12 +479,13 @@
         )
         shift = jnp.stack([query_bias, jnp.zeros_like(query_bias), value_bias])
         qkv_bf = (query_key_value + shift).astype(jnp.bfloat16)
-        kv_all = lax.all_gather(qkv_bf[:, :, 1:], "ctx", axis=1, tiled=True)
+        (kv_all,) = spread([qkv_bf[:, :, 1:].reshape(seqs, rows, 2 * cols)], "ctx", 3)
+        kv_all = jnp.transpose(kv_all, (1, 0, 2, 3)).reshape(seqs, -1, 2, cols)
         query = qkv_bf[:, :, 0].reshape(seqs, rows, heads, HEAD)
         ctx, lse = attend_forward(query, kv_all, q_pos, segment_ids, key_seg, slope)
         ctx_flat = ctx.reshape(seqs, rows, cols)
         part = jnp.einsum("slc,oc->slo", ctx_flat, w_o, preferred_element_type=jnp.float32)
-        mid = state + lax.psum(part, "mp") + vec[4]
+        mid = state + sum_mp(part) + vec[4]
         normed2, _ = norm_parts(mid)
         second_activation = (normed2 * all_gains[layer, 1] + vec[1]).astype(jnp.bfloat16)
         up_projected = (
@@ -201,7 +497,7 @@
         act, _ = gelu_parts(up_projected)
         act_bf = act.astype(jnp.bfloat16)
         down = jnp.einsum("slf,of->slo", act_bf, w_d, preferred_element_type=jnp.float32)
-        result = mid + lax.psum(down, "mp") + vec[5]
+        result = mid + sum_mp(down) + vec[5]
         return (
             result,
             (
@@ -221,7 +517,7 @@
     state = hidden_in.astype(jnp.float32)
     saves = []
     for layer in range(layers):
-        weights = (
+        weights = first_weights if layer == 0 else (
             lax.all_gather(w_qkv[layer], ("batch", "ctx"), axis=0, tiled=True),
             lax.all_gather(w_out_t[layer], ("batch", "ctx"), axis=0, tiled=True),
             lax.all_gather(w_up[layer], ("batch", "ctx"), axis=0, tiled=True),
@@ -248,13 +544,8 @@
             up_projected,
             act_bf,
         ) = saved
-        query_weight, w_o, up_weight, w_d = (
-            lax.all_gather(w_qkv[layer], ("batch", "ctx"), axis=0, tiled=True),
-            lax.all_gather(w_out_t[layer], ("batch", "ctx"), axis=0, tiled=True),
-            lax.all_gather(w_up[layer], ("batch", "ctx"), axis=0, tiled=True),
-            lax.all_gather(w_down_t[layer], ("batch", "ctx"), axis=0, tiled=True),
-        )
-        kv_all = lax.all_gather(qkv_bf[:, :, 1:], "ctx", axis=1, tiled=True)
+        query_weight, w_o, up_weight, w_d = kept_weights
+        kv_all = kv_kept
         gain1 = all_gains[layer, 0]
         gain2 = all_gains[layer, 1]
         grad_bf = grad.astype(jnp.bfloat16)
@@ -271,14 +562,13 @@
             up_gradient_half_precision,
             preferred_element_type=jnp.float32,
         )
-        da2 = lax.psum(
+        da2 = sum_mp(
             jnp.einsum(
                 "cju,xu->cjx",
                 up_gradient_half_precision,
                 up_weight,
                 preferred_element_type=jnp.float32,
-            ),
-            "mp",
+            )
         )
         normed2, inverse2 = norm_parts(mid)
         grad_g2 = jnp.sum(da2 * normed2, (0, 1))
@@ -296,7 +586,11 @@
         grad_q, grad_kv_terms = attend_backward(
             query, kv_all, q_pos, segment_ids, key_seg, slope, ctx_heads, lse, dctx_heads
         )
-        grad_kv = lax.psum_scatter(grad_kv_terms, "ctx", scatter_dimension=1, tiled=True)
+        kv_terms = jnp.transpose(
+            grad_kv_terms.astype(jnp.bfloat16).reshape(seqs, ctx_count, rows, 2 * cols),
+            (1, 0, 2, 3),
+        )
+        grad_kv = trade([kv_terms], "ctx", 4)[0].reshape(seqs, rows, 2, cols)
         grad_qf = grad_q.reshape(seqs, rows, cols)
         grad_bq = jnp.sum(grad_qf, (0, 1))
         value_bias_gradient = jnp.sum(grad_kv[:, :, 1], (0, 1))
@@ -309,14 +603,13 @@
             packed_projection_gradient,
             preferred_element_type=jnp.float32,
         )
-        da1 = lax.psum(
+        da1 = sum_mp(
             jnp.einsum(
                 "aewu,vwu->aev",
                 packed_projection_gradient,
                 query_weight,
                 preferred_element_type=jnp.float32,
-            ),
-            "mp",
+            )
         )
         normed1, inverse1 = norm_parts(x_in)
         grad_g1 = jnp.sum(da1 * normed1, (0, 1))
@@ -335,35 +628,37 @@
         )
         unit_rows = place(grad_bu, mp_index * ff_cols, full_ff).reshape(full_ff // width, width)
         bias_rows[layer] = jnp.concatenate([head_rows, unit_rows], 0)
-        matrix_grads[layer] = (
-            lax.psum_scatter(
-                query_weight_gradient.astype(jnp.bfloat16),
-                ("batch", "ctx"),
-                scatter_dimension=0,
-                tiled=True,
-            ).astype(jnp.float32),
-            lax.psum_scatter(
-                grad_wo.astype(jnp.bfloat16), ("batch", "ctx"), scatter_dimension=0, tiled=True
-            ).astype(jnp.float32),
-            lax.psum_scatter(
-                up_weight_gradient.astype(jnp.bfloat16),
-                ("batch", "ctx"),
-                scatter_dimension=0,
-                tiled=True,
-            ).astype(jnp.float32),
-            lax.psum_scatter(
-                grad_wd.astype(jnp.bfloat16), ("batch", "ctx"), scatter_dimension=0, tiled=True
-            ).astype(jnp.float32),
-        )
-    grad_gains, grad_biases = (
-        lax.psum_scatter(
-            jnp.stack(gain_rows), ("batch", "ctx", "mp"), scatter_dimension=2, tiled=True
-        ),
-        lax.psum_scatter(
-            jnp.stack(bias_rows), ("batch", "ctx", "mp"), scatter_dimension=2, tiled=True
-        ),
-    )
-    grad_qkv = jnp.stack([item[0] for item in matrix_grads])
+        rounded = [
+            item.astype(jnp.bfloat16)
+            for item in (
+                query_weight_gradient.reshape(width, 3 * cols),
+                grad_wo,
+                up_weight_gradient,
+                grad_wd,
+            )
+        ]
+        if layer:
+            matrix_grads[layer] = [
+                lax.psum_scatter(
+                    item, ("batch", "ctx"), scatter_dimension=0, tiled=True
+                ).astype(jnp.float32)
+                for item in rounded
+            ]
+    row_count = layers_rows + bias_count
+    terms = jnp.concatenate(
+        [
+            jnp.stack(gain_rows).reshape(layers_rows, width),
+            jnp.stack(bias_rows).reshape(bias_count, width),
+        ],
+        0,
+    ).reshape(row_count, owners, mp_count, part)
+    terms = jnp.transpose(terms, (2, 0, 1, 3)).reshape(mp_count, row_count, owners * part)
+    (terms,) = trade([terms], "mp", 5)
+    terms = jnp.transpose(terms.reshape(row_count, owners, part), (1, 0, 2))
+    *matrix_grads[0], terms = scatter_all(rounded + [terms.reshape(owners * row_count, part)], 6)
+    grad_gains = terms[:layers_rows].reshape(gains.shape)
+    grad_biases = terms[layers_rows:].reshape(biases.shape)
+    grad_qkv = jnp.stack([item[0] for item in matrix_grads]).reshape(w_qkv.shape)
     grad_attn_out = jnp.stack([item[1] for item in matrix_grads])
     grad_up = jnp.stack([item[2] for item in matrix_grads])
     grad_down = jnp.stack([item[3] for item in matrix_grads])

time: 1570 us -> 732 us (0.47)
  waiting for transfers between devices: 1140 us -> 15.5 us
  Pallas kernels: 0 us -> 400 us
  blocking collectives: 166 us -> 9.79 us
  local copies, waits for them, and re-layouts: 57.6 us -> 120 us
    pallas_call x0 -> x17, Pallas kernels: none -> 400 us  [the longest x8 232 us: total_mp(): pl.pallas_call(kernel, out_shape=jax.ShapeDtypeStruct((rows, width), jnp....]
    psum x7 -> x0, waiting for transfers between devices: 361 us -> none  [the longest x2 114 us: forward_layer(): result = mid + lax.psum(down, 'mp') + vec[5]]
    reduce_scatter x10 -> x3, waiting for transfers between devices: 369 us -> 15.4 us  [per_device(): lax.psum_scatter(item, ('batch', 'ctx'), scatter_dimension=0, tiled=True)]
    unnamed x29 -> x8, waiting for transfers between devices: 270 us -> 0.12 us
    all_gather x3 -> x0, blocking collectives: 147 us -> none  [the longest x1 74.2 us: per_device(): lax.all_gather(biases, ('batch', 'ctx', 'mp'), axis=2, tiled=True)]
    all_gather x2 -> x1, waiting for transfers between devices: 54.8 us -> 0.02 us  [per_device(): lax.all_gather(w_up[layer], ('batch', 'ctx'), axis=0, tiled=True)]
    all_gather x2 -> x1, waiting for transfers between devices: 54.6 us -> 0.01 us  [per_device(): lax.all_gather(w_down_t[layer], ('batch', 'ctx'), axis=0, tiled=True)]
    convert_element_type x0 -> x27, local copies, waits for them, and re-layouts: none -> 45.1 us  [the longest x6 13 us: trade(): acc = acc + got[t].astype(jnp.float32)]
  transfers between devices with their start and end apart: 27 -> 7, of which waited for: 25 -> 1; matrix products, arithmetic and copies ran while one was open for 8% -> 21% of each run, Pallas kernels for 0% -> 36%
where the time goes in v1:
time: 732 us; the launch traced here: 720 us
  Pallas kernels  400 us (55%)
  local copies, waits for them, and re-layouts  120 us (16%)
  other arithmetic  87.3 us (12%)
  matrix products  70.6 us (10%)
  between operations  16.3 us (2%)
  waiting for transfers between devices  15.5 us (2%)
  blocking collectives  9.79 us (1%)
    pallas_call x8, Pallas kernels, total_mp(): pl.pallas_call(kernel, out_shape=jax.ShapeDtypeStruct((rows, width), jnp....  232 us
    pallas_call x5, Pallas kernels, trade(): pl.pallas_call(kernel, out_shape=[jax.ShapeDtypeStruct(shape_of(a), a.dty...  84 us
    pallas_call x1, Pallas kernels, spread_all(): pl.pallas_call(kernel, out_shape=[jax.ShapeDtypeStruct((total,) + a.shape...  45.2 us
    pallas_call x3, Pallas kernels, spread(): pl.pallas_call(kernel, out_shape=[jax.ShapeDtypeStruct((count,) + a.shape...  38.9 us
    unnamed x265, local copies, waits for them, and re-layouts  17.4 us
    reduce_scatter x3, waiting for transfers between devices, per_device(): lax.psum_scatter(item, ('batch', 'ctx'), scatter_dimension=0, tiled=True)  15.4 us
  transfers between devices with their start and end apart: 7, of which 1 were waited for; matrix products, arithmetic and copies ran while one was open for 21% of the time, Pallas kernels for 36%

profile of v1, /device:TPU:0, one launch (start us, length us, event | category | flops | bytes accessed | tf_op | source)
XLA Modules:
  0.0 719.9 jit_solution(2360823011279847725)
XLA Ops:
  11.1 7.7 %spread_mp.1 = bf16[4,24,32]{2,1,0:T(8,128)(2,1)} custom-call(bf16[24,32]{1,0:T(8,128)(2,1)} %pad_maximum_fusion.12.refs_0_), custom_call_target="tpu_custom_call" | custom-call | tf_op jit(solution)/shard_map/spread_mp/pallas_call | solution.py:163
  24.0 45.2 %spread_all.1 = (bf16[8,128,768]{2,1,0:T(8,128)(2,1)}, bf16[8,128,256]{2,1,0:T(8,128)(2,1)}, bf16[8,128,1024]{2,1,0:T(8,128)(2,1)}, bf16[8,128,1024]{2,1,0:T(8,1...) custom-call(bf16[128,768]{1,0:T(8,128)(2,1)} %copy.186.refs_0_, ...), custom_call_target="tpu_custom_call" | custom-call | tf_op jit(solution)/shard_map/spread_all/pallas_call | solution.py:226
  76.2 2.6 reshape.708
  82.4 18.6 %spread_ctx.2 = bf16[4,2,128,512]{3,2,1,0:T(8,128)(2,1)} custom-call(bf16[2,128,512]{2,1,0:T(8,128)(2,1)} %bitcast.459), custom_call_target="tpu_custom_call" | custom-call | tf_op jit(solution)/shard_map/spread_ctx/pallas_call | solution.py:163
  108.7 27.0 %total_mp.8 = bf16[256,1024]{1,0:T(8,128)(2,1)} custom-call(bf16[256,1024]{1,0:T(8,128)(2,1)} %convolution_convert_fusion.3.x_ref), custom_call_target="tpu_custom_call" | custom-call | tf_op jit(solution)/shard_map/total_mp/pallas_call | solution.py:124
  138.8 3.7 multiply_convert_fusion.3
  144.9 30.2 %total_mp.9 = bf16[256,1024]{1,0:T(8,128)(2,1)} custom-call(bf16[256,1024]{1,0:T(8,128)(2,1)} %convolution_convert_fusion.5.x_ref), custom_call_target="tpu_custom_call" | custom-call | tf_op jit(solution)/shard_map/total_mp/pallas_call | solution.py:124
  180.1 9.8 %all-gather.1 = bf16[1,1024,256]{2,1,0:T(8,128)(2,1)S(1)} all-gather(bf16[1,128,256]{2,1,0:T(8,128)(2,1)S(1)} %get-tuple-element.139), channel_id=3, replica_groups=mesh['batch'=2,'ctx'=4,'mp'=4] {'batch','ctx'}, dimensions={1}, use_global_device_ids=true | all-gather | bytes 589824 | tf_op jit(solution)/shard_map/all_gather | solution.py:522
  193.2 12.7 %spread_ctx.3 = bf16[4,2,128,512]{3,2,1,0:T(8,128)(2,1)} custom-call(bf16[2,128,512]{2,1,0:T(8,128)(2,1)} %bitcast.460), custom_call_target="tpu_custom_call" | custom-call | tf_op jit(solution)/shard_map/spread_ctx/pallas_call | solution.py:163
  207.0 2.7 copy.200
  209.7 2.3 reshape_reshape.12
  212.2 2.5 fusion.20
  217.4 28.4 %total_mp.10 = bf16[256,1024]{1,0:T(8,128)(2,1)} custom-call(bf16[256,1024]{1,0:T(8,128)(2,1)} %convolution_convert_fusion.2.x_ref), custom_call_target="tpu_custom_call" | custom-call | tf_op jit(solution)/shard_map/total_mp/pallas_call | solution.py:124
  247.4 3.4 fusion.25
  250.8 3.5 fusion.40
  254.3 30.2 %total_mp.11 = bf16[256,1024]{1,0:T(8,128)(2,1)} custom-call(bf16[256,1024]{1,0:T(8,128)(2,1)} %bitcast.473), custom_call_target="tpu_custom_call" | custom-call | tf_op jit(solution)/shard_map/total_mp/pallas_call | solution.py:124
  284.5 3.9 fusion.167
  290.8 28.7 %total_mp.12 = bf16[256,1024]{1,0:T(8,128)(2,1)} custom-call(bf16[256,1024]{1,0:T(8,128)(2,1)} %bitcast.471), custom_call_target="tpu_custom_call" | custom-call | tf_op jit(solution)/shard_map/total_mp/pallas_call | solution.py:124
  321.6 2.2 multiply_reduce_fusion
  329.0 3.1 multiply_convert_fusion.1
  336.6 3.6 copy.206
  340.2 3.6 copy.207
  343.7 4.3 pad_maximum_fusion
  348.1 2.6 convert_element_type.610
  350.7 2.3 copy.317
  355.5 13.7 %trade_ctx.2 = bf16[3,2,128,512]{3,2,1,0:T(8,128)(2,1)} custom-call(bf16[4,2,128,512]{3,2,1,0:T(8,128)(2,1)} %bitcast.441), custom_call_target="tpu_custom_call" | custom-call | tf_op jit(solution)/shard_map/trade_ctx/pallas_call | solution.py:266
  369.2 2.3 slice_convert_fusion.5
  371.5 2.2 reshape.746
  373.7 2.2 reshape.747
  382.2 2.6 fusion.154
  386.8 28.4 %total_mp.13 = bf16[256,1024]{1,0:T(8,128)(2,1)} custom-call(bf16[256,1024]{1,0:T(8,128)(2,1)} %bitcast.472), custom_call_target="tpu_custom_call" | custom-call | tf_op jit(solution)/shard_map/total_mp/pallas_call | solution.py:124
  417.3 2.2 multiply_reduce_fusion.1
  425.6 30.2 %total_mp.14 = bf16[256,1024]{1,0:T(8,128)(2,1)} custom-call(bf16[256,1024]{1,0:T(8,128)(2,1)} %convolution_convert_fusion.4.x_ref), custom_call_target="tpu_custom_call" | custom-call | tf_op jit(solution)/shard_map/total_mp/pallas_call | solution.py:124
  457.8 2.5 multiply_reduce_fusion.2
  464.5 3.1 multiply_convert_fusion
  472.2 3.6 copy.216
  475.8 3.6 copy.217
  479.3 4.2 pad_maximum_fusion.1
  483.5 2.7 convert_element_type.636
  486.2 2.3 copy.316
  491.1 12.5 %trade_ctx.3 = bf16[3,2,128,512]{3,2,1,0:T(8,128)(2,1)} custom-call(bf16[4,2,128,512]{3,2,1,0:T(8,128)(2,1)} %bitcast.440), custom_call_target="tpu_custom_call" | custom-call | tf_op jit(solution)/shard_map/trade_ctx/pallas_call | solution.py:266
  503.6 2.3 slice_convert_fusion.2
  505.9 2.2 reshape.752
  508.1 2.2 reshape.753
  516.5 2.4 fusion.46
  519.0 2.6 fusion.153
  523.8 28.4 %total_mp.15 = bf16[256,1024]{1,0:T(8,128)(2,1)} custom-call(bf16[256,1024]{1,0:T(8,128)(2,1)} %fusion.33.x_ref), custom_call_target="tpu_custom_call" | custom-call | tf_op jit(solution)/shard_map/total_mp/pallas_call | solution.py:124
  554.9 2.9 bitcast_convert_fusion.4
  557.8 2.7 copy.270
  572.8 3.6 fusion.10
  580.1 9.7 %trade_mp.1 = f32[3,24,256]{2,1,0:T(8,128)} custom-call(f32[4,24,256]{2,1,0:T(8,128)} %reshape.720.refs_0_), custom_call_target="tpu_custom_call" | custom-call | tf_op jit(solution)/shard_map/trade_mp/pallas_call | solution.py:266
  593.2 2.6 copy.229
  595.8 3.8 convert_element_type.651
  599.6 5.1 copy.234.refs_0_
  605.9 3.2 bitcast_convert_fusion.2
  609.1 2.3 bitcast_convert_fusion.3
  611.4 6.5 trade_core.1
  621.3 3.0 fusion.refs_3_
  625.8 2.2 bitcast_convert_fusion.1
  628.0 4.2 constant_dynamic-slice_fusion
  632.2 3.4 copy.277
  635.7 2.2 fusion.11.refs_0_
  637.9 41.6 %trade_chip.1 = (bf16[3,128,768]{2,1,0:T(8,128)(2,1)}, bf16[3,128,256]{2,1,0:T(8,128)(2,1)}, bf16[3,128,1024]{2,1,0:T(8,128)(2,1)}, bf16[3,128,1024]{2,1,0:T(8,128)(2,1)}, f32[3,24,32]{2,1,0:T(8,128)}) custom-call(bf16[4,128,768]{2,1,0:T(8,128)(2,1)} %fusion.11.refs_0_, bf16[4,128,256]{2,1,0:T(8,128)(2,1)} %fusion.114.refs_1_, ...), custom_call_target="tpu_custom_call" | custom-call | tf_op jit(solution)/shard_map/trade_chip/pallas_call | solution.py:266
  695.2 15.4 %reduce-scatter.9.cloned.1.call-done = bf16[128,1024]{1,0:T(8,128)(2,1)} async-done(((bf16[1024,1024]{1,0:T(8,128)(2,1)}), bf16[128,1024]{1,0:T(8,128)(2,1)}) %reduce-scatter.9.cloned.1.call-update) | async-done | bytes 262160 | tf_op jit(solution)/shard_map/reduce_scatter | solution.py:642
  (489 shorter events, 146.4 us)
Async XLA Ops:
  7.2 15.4 %copy-start.30 = (bf16[2,128,1024]{2,1,0:T(8,128)(2,1)S(1)}, bf16[2,128,1024]{2,1,0:T(8,128)(2,1)}, u32[]{:S(2)}) copy-start(bf16[2,128,1024]{2,1,0:T(8,128)(2,1)} %param.16) | copy-start | bytes 1572868
  7.2 16.1 %copy-start.29 = (bf16[2,128,1024]{2,1,0:T(8,128)(2,1)S(1)}, bf16[2,128,1024]{2,1,0:T(8,128)(2,1)}, u32[]{:S(2)}) copy-start(bf16[2,128,1024]{2,1,0:T(8,128)(2,1)} %param.15) | copy-start | bytes 1572868
  7.2 183.0 %all-gather.8.cloned.1.call-start = ((), (), s32[]{:S(2)}) async-start(), calls=%async_computation.7 | async-start | bytes 1769472 | tf_op jit(solution)/shard_map/all_gather | solution.py:521
  9.1 238.4 %all-gather.10.cloned.1.call-start = ((), (), s32[]{:S(2)}) async-start(), calls=%async_computation.8 | async-start | bytes 2359296 | tf_op jit(solution)/shard_map/all_gather | solution.py:523
  23.3 47.8 %copy-start.55 = (bf16[4,24,32]{2,1,0:T(8,128)(2,1)S(1)}, bf16[4,24,32]{2,1,0:T(8,128)(2,1)}, u32[]{:S(2)}) copy-start(bf16[4,24,32]{2,1,0:T(8,128)(2,1)} %constant_dynamic-update-slice_fusion.8) | copy-start | bytes 18436
  69.2 4.9 copy-start.28
  70.1 180.7 %all-gather.12.cloned.1.call-start = ((), (), s32[]{:S(2)}) async-start(), calls=%async_computation.9 | async-start | bytes 2359296 | tf_op jit(solution)/shard_map/all_gather | solution.py:524
  71.0 617.3 %reduce-scatter.7.cloned.1.call-start = ((), (), s32[]{:S(2)}) async-start(), calls=%async_computation.4 | async-start | bytes 589824 | tf_op jit(solution)/shard_map/reduce_scatter | solution.py:642
  73.3 6.8 copy-start.103
  80.8 20.7 %copy-start.43 = (bf16[2,128,3,256]{3,1,2,0:T(8,128)(2,1)}, bf16[2,128,3,256]{3,1,2,0:T(8,128)(2,1)S(1)}, u32[]{:S(2)}) copy-start(bf16[2,128,3,256]{3,1,2,0:T(8,128)(2,1)S(1)} %fusion.56) | copy-start | bytes 1179652
  104.8 110.5 %copy-start.58 = (pred[2,128,512]{2,1,0:T(8,128)(4,1)}, pred[2,128,512]{2,1,0:T(8,128)(4,1)S(1)}, u32[]{:S(2)}) copy-start(pred[2,128,512]{2,1,0:T(8,128)(4,1)S(1)} %compare_and_fusion) | copy-start | bytes 393220
  107.3 28.5 %copy-start.70 = (f32[1,8,4,32]{3,2,1,0:T(4,128)S(1)}, f32[1,8,4,32]{3,2,1,0:T(4,128)}, u32[]{:S(2)}) copy-start(f32[1,8,4,32]{3,2,1,0:T(4,128)} %get-tuple-element.132) | copy-start | bytes 12292
  107.6 31.0 %copy-start.63 = (bf16[4,8,4,32]{3,2,1,0:T(4,128)(2,1)S(1)}, bf16[4,8,4,32]{3,2,1,0:T(4,128)(2,1)}, u32[]{:S(2)}) copy-start(bf16[4,8,4,32]{3,2,1,0:T(4,128)(2,1)} %get-tuple-element.137) | copy-start | bytes 24580
  107.6 31.1 %copy-start.69 = (f32[1,8,4,32]{3,2,1,0:T(4,128)S(1)}, f32[1,8,4,32]{3,2,1,0:T(4,128)}, u32[]{:S(2)}) copy-start(f32[1,8,4,32]{3,2,1,0:T(4,128)} %get-tuple-element.131) | copy-start | bytes 12292
  137.2 5.3 copy-start.87
  138.8 4.5 copy-start.118
  143.3 31.8 %copy-start.68 = (f32[1,8,4,32]{3,2,1,0:T(4,128)S(1)}, f32[1,8,4,32]{3,2,1,0:T(4,128)}, u32[]{:S(2)}) copy-start(f32[1,8,4,32]{3,2,1,0:T(4,128)} %get-tuple-element.130) | copy-start | bytes 12292
  144.9 32.3 %copy-start.67 = (f32[1,8,4,32]{3,2,1,0:T(4,128)S(1)}, f32[1,8,4,32]{3,2,1,0:T(4,128)}, u32[]{:S(2)}) copy-start(f32[1,8,4,32]{3,2,1,0:T(4,128)} %get-tuple-element.129) | copy-start | bytes 12292
  144.9 32.4 %copy-start.66 = (f32[1,8,4,32]{3,2,1,0:T(4,128)S(1)}, f32[1,8,4,32]{3,2,1,0:T(4,128)}, u32[]{:S(2)}) copy-start(f32[1,8,4,32]{3,2,1,0:T(4,128)} %get-tuple-element.126) | copy-start | bytes 12292
  144.9 33.0 %copy-start.62 = (bf16[4,8,4,32]{3,2,1,0:T(4,128)(2,1)S(1)}, bf16[4,8,4,32]{3,2,1,0:T(4,128)(2,1)}, u32[]{:S(2)}) copy-start(bf16[4,8,4,32]{3,2,1,0:T(4,128)(2,1)} %get-tuple-element.136) | copy-start | bytes 24580
  144.9 33.1 %copy-start.65 = (f32[1,8,4,32]{3,2,1,0:T(4,128)S(1)}, f32[1,8,4,32]{3,2,1,0:T(4,128)}, u32[]{:S(2)}) copy-start(f32[1,8,4,32]{3,2,1,0:T(4,128)} %get-tuple-element.125) | copy-start | bytes 12292
  144.9 33.8 %copy-start.64 = (f32[1,8,4,32]{3,2,1,0:T(4,128)S(1)}, f32[1,8,4,32]{3,2,1,0:T(4,128)}, u32[]{:S(2)}) copy-start(f32[1,8,4,32]{3,2,1,0:T(4,128)} %get-tuple-element.124) | copy-start | bytes 12292
  176.6 13.7 %copy-start.72 = (f32[1,1,1024]{2,1,0:T(1,128)S(1)}, f32[1,1,1024]{2,1,0:T(1,128)}, u32[]{:S(2)}) copy-start(f32[1,1,1024]{2,1,0:T(1,128)} %get-tuple-element.142) | copy-start | bytes 12292
  176.6 13.7 %copy-start.108 = (f32[3,256]{1,0:T(4,128)S(1)}, f32[3,256]{1,0:T(4,128)}, u32[]{:S(2)}) copy-start(f32[3,256]{1,0:T(4,128)} %get-tuple-element.145) | copy-start | bytes 9220
  177.3 15.0 %copy-start.107 = (f32[1024]{0:T(1024)}, f32[1024]{0:T(1024)S(1)}, u32[]{:S(2)}) copy-start(f32[1024]{0:T(1024)S(1)} %reshape.737) | copy-start | bytes 12292
  189.9 26.4 %copy-start.17 = (bf16[1,1024,256]{2,1,0:T(8,128)(2,1)}, bf16[1,1024,256]{2,1,0:T(8,128)(2,1)S(1)}, u32[]{:S(2)}) copy-start(bf16[1,1024,256]{2,1,0:T(8,128)(2,1)S(1)} %all-gather.1) | copy-start | bytes 1572868
  207.0 5.0 slice-start.1
  216.1 29.7 %copy-start.84 = (f32[1024]{0:T(1024)S(1)}, f32[1024]{0:T(1024)}, u32[]{:S(2)}) copy-start(f32[1024]{0:T(1024)} %reshape.739) | copy-start | bytes 12292
  247.1 76.7 %copy-start.74 = (f32[2,128]{1,0:T(2,128)}, f32[2,128]{1,0:T(2,128)S(1)}, u32[]{:S(2)}) copy-start(f32[2,128]{1,0:T(2,128)S(1)} %broadcast_multiply_fusion.5) | copy-start | bytes 3076
  247.4 76.5 %copy-start.79 = (f32[2,128]{1,0:T(2,128)}, f32[2,128]{1,0:T(2,128)S(1)}, u32[]{:S(2)}) copy-start(f32[2,128]{1,0:T(2,128)S(1)} %add_rsqrt_fusion) | copy-start | bytes 3076
  284.5 4.7 copy-start.117
  290.8 33.0 %copy-start.83 = (f32[1024]{0:T(1024)S(1)}, f32[1024]{0:T(1024)}, u32[]{:S(2)}) copy-start(f32[1024]{0:T(1024)} %reshape.743) | copy-start | bytes 12292
  329.0 4.8 copy-start.49
  348.1 6.6 copy-start.51
  380.1 5.4 copy-start.61
  386.8 32.7 %copy-start.73 = (f32[1,1,1024]{2,1,0:T(1,128)S(1)}, f32[1,1,1024]{2,1,0:T(1,128)}, u32[]{:S(2)}) copy-start(f32[1,1,1024]{2,1,0:T(1,128)} %get-tuple-element.142) | copy-start | bytes 12292
  386.8 32.7 %copy-start.91 = (f32[2,128]{1,0:T(2,128)S(1)}, f32[2,128]{1,0:T(2,128)}, u32[]{:S(2)}) copy-start(f32[2,128]{1,0:T(2,128)} %copy-done.90) | copy-start | bytes 3076
  386.8 32.7 %copy-start.100 = (f32[2,128]{1,0:T(2,128)S(1)}, f32[2,128]{1,0:T(2,128)}, u32[]{:S(2)}) copy-start(f32[2,128]{1,0:T(2,128)} %copy-done.99) | copy-start | bytes 3076
  415.3 4.3 copy-start.5
  424.0 33.8 %copy-start.88 = (f32[2,128]{1,0:T(2,128)S(1)}, f32[2,128]{1,0:T(2,128)}, u32[]{:S(2)}) copy-start(f32[2,128]{1,0:T(2,128)} %copy-done.87) | copy-start | bytes 3076
  424.0 33.8 %copy-start.97 = (f32[2,128]{1,0:T(2,128)S(1)}, f32[2,128]{1,0:T(2,128)}, u32[]{:S(2)}) copy-start(f32[2,128]{1,0:T(2,128)} %copy-done.96) | copy-start | bytes 3076
  455.8 4.6 copy-start.10
  455.8 4.6 copy-start.12
  464.5 4.8 copy-start.47
  483.5 6.8 copy-start.50
  518.9 171.9 %reduce-scatter.13.cloned.1.call-start = ((), (), s32[]{:S(2)}) async-start(), calls=%async_computation.10 | async-start | bytes 1769472
  557.8 6.1 copy-start.7
  560.5 8.0 %copy-start.31 = (f32[2,128,2,256]{3,1,2,0:T(8,128)S(1)}, f32[2,128,2,256]{3,1,2,0:T(8,128)}, u32[]{:S(2)}) copy-start(f32[2,128,2,256]{3,1,2,0:T(8,128)} %get-tuple-element.97) | copy-start | bytes 1572868
  565.7 127.5 %reduce-scatter.11.cloned.1.call-start = ((), (), s32[]{:S(2)}) async-start(), calls=%async_computation.6 | async-start | bytes 2359296 | tf_op jit(solution)/shard_map/reduce_scatter | solution.py:642
  576.4 14.9 %copy-start.45 = (bf16[2,128,1,256]{3,1,0,2:T(8,128)(2,1)S(1)}, bf16[2,128,1,256]{3,1,0,2:T(8,128)(2,1)}, u32[]{:S(2)}) copy-start(bf16[2,128,1,256]{3,1,0,2:T(8,128)(2,1)} %copy.224) | copy-start | bytes 393220
  576.4 14.9 %copy-start.77 = (f32[2,128]{1,0:T(2,128)S(1)}, f32[2,128]{1,0:T(2,128)}, u32[]{:S(2)}) copy-start(f32[2,128]{1,0:T(2,128)} %copy-done.76) | copy-start | bytes 3076
  576.4 14.9 %copy-start.93 = (f32[2,128]{1,0:T(2,128)S(1)}, f32[2,128]{1,0:T(2,128)}, u32[]{:S(2)}) copy-start(f32[2,128]{1,0:T(2,128)} %copy-done.92) | copy-start | bytes 3076
  576.4 14.9 %copy-start.104 = (f32[1024]{0:T(1024)S(1)}, f32[1024]{0:T(1024)}, u32[]{:S(2)}) copy-start(f32[1024]{0:T(1024)} %copy-done.103) | copy-start | bytes 12292
  576.4 134.2 %reduce-scatter.9.cloned.1.call-start = ((), (), s32[]{:S(2)}) async-start(), calls=%async_computation.5 | async-start | bytes 2359296 | tf_op jit(solution)/shard_map/reduce_scatter | solution.py:642
  599.6 5.1 copy-start.3
  611.4 6.6 copy-start.38
  611.4 8.2 %copy-start.19 = (bf16[1024,256]{1,0:T(8,128)(2,1)S(1)}, bf16[1024,256]{1,0:T(8,128)(2,1)}, u32[]{:S(2)}) copy-start(bf16[1024,256]{1,0:T(8,128)(2,1)} %fusion.45) | copy-start | bytes 1572868
  617.9 6.4 copy-start.16
  618.0 6.4 copy-start.36
  637.9 45.2 %copy-start.101 = (f32[256]{0:T(256)S(1)}, f32[256]{0:T(256)}, u32[]{:S(2)}) copy-start(f32[256]{0:T(256)} %get-tuple-element.83) | copy-start | bytes 3076
  637.9 45.2 %copy-start.115 = (f32[2,128]{1,0:T(2,128)S(1)}, f32[2,128]{1,0:T(2,128)}, u32[]{:S(2)}) copy-start(f32[2,128]{1,0:T(2,128)} %get-tuple-element.79) | copy-start | bytes 3076
  682.2 4.9 copy-start.8
  682.2 4.9 copy-start.78
  682.2 4.9 copy-start.94
  (74 other events, 165.0 us)
Sparse Core Ops, SparseCore 0:
  9.9 33.8 all-gather.7
  70.2 32.8 all-gather.9
  105.0 27.6 all-gather.11
  519.0 37.5 reduce-scatter.6
  565.8 41.8 reduce-scatter.12
  610.8 55.0 reduce-scatter.10
  669.3 41.2 reduce-scatter.8

commit v2 on v1

--- a/solution.py
+++ b/solution.py
@@ -83,16 +83,41 @@
     )
 
 
-def total_mp(values, name):
+def pick(ref, rank, dim):
+    return ref.at[rank] if dim == 0 else ref.at[:, rank]
+
+
+def cut(shape, dim):
+    return shape[:dim] + shape[dim + 1 :]
+
+
+def gathered(got, own, kind, dim):
+    acc = lax.dynamic_index_in_dim(own, rank_of(kind)[0], dim, keepdims=False)
+    acc = acc.astype(jnp.float32)
+    for t in range(got.shape[0]):
+        acc = acc + got[t].astype(jnp.float32)
+    return acc
+
+
+def total_mp(values, riders=(), ident=0):
     rows, width = values.shape
+    size = len(riders)
+    extra = [rank_of(kind)[1] - 1 for _, kind, _ in riders]
     count = lax.axis_size("mp")
     piece = rows // count
 
-    def kernel(x_ref, o_ref, held, send, recv):
+    def kernel(x_ref, *refs):
+        loads, o_ref, lands = refs[:size], refs[size], refs[size + 1 : 2 * size + 1]
+        held, send, recv, *pairs = refs[2 * size + 1 :]
         me, _ = rank_of("mp")
         ranks = [lax.rem(me + t, count) for t in range(1, count)]
         devices = [device_of("mp", rank) for rank in ranks]
-        greet(devices)
+        targets = {}
+        for kind in sorted({kind for _, kind, _ in riders}):
+            own, many = rank_of(kind)
+            peers = [lax.rem(own + t, many) for t in range(1, many)]
+            targets[kind] = [(peer, device_of(kind, peer)) for peer in peers]
+        greet(devices + [d for group in targets.values() for _, d in group])
         mine = pl.ds(pl.multiple_of(me * piece, piece), piece)
         first = []
         for t in range(count - 1):
@@ -100,6 +125,15 @@
             copy = remote(x_ref.at[theirs], held.at[t], send.at[0, t], recv.at[0, t], devices[t])
             copy.start()
             first.append(copy)
+        carried = []
+        for i, (_, kind, dim) in enumerate(riders):
+            for t, (peer, device) in enumerate(targets[kind]):
+                copy = remote(
+                    pick(loads[i], peer, dim), lands[i].at[t],
+                    pairs[2 * i].at[t], pairs[2 * i + 1].at[t], device,
+                )
+                copy.start()
+                carried.append(copy)
         acc = x_ref[mine, :].astype(jnp.float32)
         for t in range(count - 1):
             first[t].wait_recv()
@@ -120,23 +154,31 @@
             remote(
                 o_ref.at[theirs], o_ref.at[theirs], send.at[1, t], recv.at[1, t], devices[t]
             ).wait_recv()
-
-    return pl.pallas_call(
+        for copy in carried:
+            copy.wait()
+
+    total, *outs = pl.pallas_call(
         kernel,
-        out_shape=jax.ShapeDtypeStruct((rows, width), jnp.bfloat16),
-        in_specs=[VMEM],
-        out_specs=VMEM,
+        out_shape=[jax.ShapeDtypeStruct((rows, width), jnp.bfloat16)]
+        + [
+            jax.ShapeDtypeStruct((many,) + cut(a.shape, dim), a.dtype)
+            for (a, _, dim), many in zip(riders, extra)
+        ],
+        in_specs=[VMEM] + [ANY] * size,
+        out_specs=[VMEM] + [ANY] * size,
         scratch_shapes=[
             pltpu.VMEM((count - 1, piece, width), jnp.bfloat16),
             pltpu.SemaphoreType.DMA((2, count - 1)),
             pltpu.SemaphoreType.DMA((2, count - 1)),
-        ],
-        compiler_params=pltpu.CompilerParams(collective_id=0, has_side_effects=True),
+        ]
+        + [pltpu.SemaphoreType.DMA((many,)) for many in extra for _ in range(2)],
+        compiler_params=pltpu.CompilerParams(collective_id=ident, has_side_effects=True),
         name="total_mp",
-    )(values)
-
-
-def spread(arrays, kind, ident):
+    )(values, *[a for a, _, _ in riders])
+    return total, [gathered(o, *rider) for o, rider in zip(outs, riders)]
+
+
+def spread(arrays, kind, ident, dim=0):
     me, count = rank_of(kind)
     size = len(arrays)
 
@@ -148,7 +190,7 @@
         copies = []
         for t in range(count - 1):
             for i in range(size):
-                copy = remote(ins[i], outs[i].at[rank], send.at[i, t], recv.at[i, t], devices[t])
+                copy = remote(ins[i], pick(outs[i], rank, dim), send.at[i, t], recv.at[i, t], devices[t])
                 copy.start()
                 copies.append(copy)
         for copy in copies:
@@ -157,19 +199,21 @@
             source = lax.rem(rank + count - 1 - t, count)
             for i in range(size):
                 remote(
-                    ins[i], outs[i].at[source], send.at[i, t], recv.at[i, t], devices[t]
+                    ins[i], pick(outs[i], source, dim), send.at[i, t], recv.at[i, t], devices[t]
                 ).wait_recv()
 
     outs = pl.pallas_call(
         kernel,
-        out_shape=[jax.ShapeDtypeStruct((count,) + a.shape, a.dtype) for a in arrays],
+        out_shape=[
+            jax.ShapeDtypeStruct(a.shape[:dim] + (count,) + a.shape[dim:], a.dtype) for a in arrays
+        ],
         in_specs=[ANY] * size,
         out_specs=[ANY] * size,
         scratch_shapes=[pltpu.SemaphoreType.DMA((size, count - 1))] * 2,
         compiler_params=pltpu.CompilerParams(collective_id=ident, has_side_effects=True),
         name="spread_" + kind,
     )(*arrays)
-    return [lax.dynamic_update_index_in_dim(o, a, me, 0) for o, a in zip(outs, arrays)]
+    return [lax.dynamic_update_index_in_dim(o, a, me, dim) for o, a in zip(outs, arrays)]
 
 
 def spread_all(arrays, ident):
@@ -237,11 +281,8 @@
 
 
 def trade(arrays, kind, ident, dim=0):
-    me, count = rank_of(kind)
+    _, count = rank_of(kind)
     size = len(arrays)
-
-    def pick(ref, rank):
-        return ref.at[rank] if dim == 0 else ref.at[:, rank]
 
     def kernel(*refs):
         ins, outs, (send, recv) = refs[:size], refs[size : 2 * size], refs[2 * size :]
@@ -253,39 +294,23 @@
         for t in range(count - 1):
             for i in range(size):
                 copy = remote(
-                    pick(ins[i], ranks[t]), outs[i].at[t], send.at[i, t], recv.at[i, t], devices[t]
+                    pick(ins[i], ranks[t], dim), outs[i].at[t], send.at[i, t], recv.at[i, t], devices[t]
                 )
                 copy.start()
                 copies.append(copy)
         for copy in copies:
             copy.wait()
 
-    def shape_of(a):
-        return (count - 1,) + a.shape[:dim] + a.shape[dim + 1 :]
-
     outs = pl.pallas_call(
         kernel,
-        out_shape=[jax.ShapeDtypeStruct(shape_of(a), a.dtype) for a in arrays],
+        out_shape=[jax.ShapeDtypeStruct((count - 1,) + cut(a.shape, dim), a.dtype) for a in arrays],
         in_specs=[ANY] * size,
         out_specs=[ANY] * size,
         scratch_shapes=[pltpu.SemaphoreType.DMA((size, count - 1))] * 2,
         compiler_params=pltpu.CompilerParams(collective_id=ident, has_side_effects=True),
         name="trade_" + kind,
     )(*arrays)
-    sums = []
-    for got, a in zip(outs, arrays):
-        acc = lax.dynamic_index_in_dim(a, me, dim, keepdims=False).astype(jnp.float32)
-        for t in range(count - 1):
-            acc = acc + got[t].astype(jnp.float32)
-        sums.append(acc)
-    return sums
-
-
-def scatter_all(arrays, ident):
-    _, total = rank_of("flat")
-    split = [a.reshape((total // 2, 2, a.shape[0] // total) + a.shape[1:]) for a in arrays]
-    halves = trade(split, "core", ident, dim=1)
-    return trade([h.astype(a.dtype) for h, a in zip(halves, arrays)], "chip", ident + 1)
+    return [gathered(o, a, kind, dim) for o, a in zip(outs, arrays)]
 
 
 def block_mask(q_pos, q_seg, key_seg, start, block):
@@ -304,9 +329,9 @@
     return score * scale - slope[None, :, None, None] * dist[None, None]
 
 
-def attend_forward(query, kv_all, q_pos, q_seg, key_seg, slope):
+def attend_forward(query, keys, values, q_pos, q_seg, key_seg, slope):
     seqs, rows, heads, width = query.shape
-    length = kv_all.shape[1]
+    length = keys.shape[1]
     block = min(512, length)
     scale = 1.0 / math.sqrt(width)
 
@@ -316,15 +341,14 @@
 
         def work(state):
             acc, total = state
-            pair = lax.dynamic_slice_in_dim(kv_all, start, block, 1).reshape(
-                seqs, block, 2, heads, width
-            )
-            score = block_scores(query, pair[:, :, 0], q_pos, start, block, slope, scale)
+            key_part = lax.dynamic_slice_in_dim(keys, start, block, 1)
+            value_part = lax.dynamic_slice_in_dim(values, start, block, 1)
+            score = block_scores(query, key_part, q_pos, start, block, slope, scale)
             expo = jnp.where(mask, jnp.exp(jnp.where(mask, score, 0.0)), 0.0)
             acc = acc + jnp.einsum(
                 "shqk,skhd->sqhd",
                 expo.astype(jnp.bfloat16),
-                pair[:, :, 1],
+                value_part,
                 preferred_element_type=jnp.float32,
             )
             return (acc, total + jnp.sum(expo, -1))
@@ -342,9 +366,9 @@
     return (ctx, jnp.log(total))
 
 
-def attend_backward(query, kv_all, q_pos, q_seg, key_seg, slope, ctx, lse, dctx):
+def attend_backward(query, keys, values, q_pos, q_seg, key_seg, slope, ctx, lse, dctx):
     seqs, rows, heads, width = query.shape
-    length = kv_all.shape[1]
+    length = keys.shape[1]
     block = min(512, length)
     scale = 1.0 / math.sqrt(width)
     delta = jnp.transpose(
@@ -356,11 +380,10 @@
         mask = block_mask(q_pos, q_seg, key_seg, start, block)
 
         def work(state):
-            grad_q, grad_kv = state
-            pair = lax.dynamic_slice_in_dim(kv_all, start, block, 1).reshape(
-                seqs, block, 2, heads, width
-            )
-            score = block_scores(query, pair[:, :, 0], q_pos, start, block, slope, scale)
+            grad_q, grad_keys, grad_values = state
+            key_part = lax.dynamic_slice_in_dim(keys, start, block, 1)
+            value_part = lax.dynamic_slice_in_dim(values, start, block, 1)
+            score = block_scores(query, key_part, q_pos, start, block, slope, scale)
             prob = jnp.where(mask, jnp.exp(jnp.where(mask, score - lse[..., None], 0.0)), 0.0)
             grad_v = jnp.einsum(
                 "shqk,sqhd->skhd",
@@ -369,13 +392,13 @@
                 preferred_element_type=jnp.float32,
             )
             grad_p = jnp.einsum(
-                "sqhd,skhd->shqk", dctx, pair[:, :, 1], preferred_element_type=jnp.float32
+                "sqhd,skhd->shqk", dctx, value_part, preferred_element_type=jnp.float32
             )
             grad_s = (prob * (grad_p - delta[..., None])).astype(jnp.bfloat16)
             grad_q = (
                 grad_q
                 + jnp.einsum(
-                    "shqk,skhd->sqhd", grad_s, pair[:, :, 0], preferred_element_type=jnp.float32
+                    "shqk,skhd->sqhd", grad_s, key_part, preferred_element_type=jnp.float32
                 )
                 * scale
             )
@@ -383,10 +406,13 @@
                 jnp.einsum("shqk,sqhd->skhd", grad_s, query, preferred_element_type=jnp.float32)
                 * scale
             )
-            piece = jnp.stack([grad_k, grad_v], 2).reshape(seqs, block, 2, heads * width)
             if length == block:
-                return (grad_q, piece)
-            return (grad_q, lax.dynamic_update_slice_in_dim(grad_kv, piece, start, 1))
+                return (grad_q, grad_k, grad_v)
+            return (
+                grad_q,
+                lax.dynamic_update_slice_in_dim(grad_keys, grad_k, start, 1),
+                lax.dynamic_update_slice_in_dim(grad_values, grad_v, start, 1),
+            )
 
         if length == block:
             return (work(carry), None)
@@ -394,13 +420,14 @@
 
     init = (
         jnp.zeros(query.shape, jnp.float32),
-        jnp.zeros((seqs, length, 2, heads * width), jnp.float32),
+        jnp.zeros(keys.shape, jnp.float32),
+        jnp.zeros(keys.shape, jnp.float32),
     )
     if length == block:
-        (grad_q, grad_kv), _ = step(init, 0)
+        grads, _ = step(init, 0)
     else:
-        (grad_q, grad_kv), _ = lax.scan(step, init, jnp.arange(length // block, dtype=jnp.int32))
-    return (grad_q, grad_kv)
+        grads, _ = lax.scan(step, init, jnp.arange(length // block, dtype=jnp.int32))
+    return grads
 
 
 def per_device(hidden_in, segment_ids, gains, biases, w_qkv, w_out_t, w_up, w_down_t, grad_out):
@@ -447,9 +474,26 @@
         first[3].reshape(width, ff_cols),
     )
 
+    def ride_mp(values, riders=(), ident=0):
+        flat = values.reshape(seqs * rows, width).astype(jnp.bfloat16)
+        total, sums = total_mp(flat, riders, ident)
+        return total.reshape(values.shape).astype(jnp.float32), sums
+
     def sum_mp(values):
-        flat = values.reshape(seqs * rows, width).astype(jnp.bfloat16)
-        return total_mp(flat, "mp").reshape(values.shape).astype(jnp.float32)
+        return ride_mp(values)[0]
+
+    def core_riders(arrays):
+        return [
+            (
+                a.astype(jnp.bfloat16).reshape(owners // 2, 2, width // owners, a.shape[1]),
+                "core",
+                1,
+            )
+            for a in arrays
+        ]
+
+    def chip_riders(arrays):
+        return [(a.astype(jnp.bfloat16), "chip", 0) for a in arrays]
 
     q_pos = lax.axis_index("ctx") * rows + jnp.arange(rows, dtype=jnp.int32)
     head_ids = (mp_index * heads + jnp.arange(heads, dtype=jnp.int32)).astype(jnp.float32)
@@ -479,10 +523,12 @@
         )
         shift = jnp.stack([query_bias, jnp.zeros_like(query_bias), value_bias])
         qkv_bf = (query_key_value + shift).astype(jnp.bfloat16)
-        (kv_all,) = spread([qkv_bf[:, :, 1:].reshape(seqs, rows, 2 * cols)], "ctx", 3)
-        kv_all = jnp.transpose(kv_all, (1, 0, 2, 3)).reshape(seqs, -1, 2, cols)
+        kv_all = [
+            item.reshape(seqs, -1, heads, HEAD)
+            for item in spread([qkv_bf[:, :, 1], qkv_bf[:, :, 2]], "ctx", 3, 1)
+        ]
         query = qkv_bf[:, :, 0].reshape(seqs, rows, heads, HEAD)
-        ctx, lse = attend_forward(query, kv_all, q_pos, segment_ids, key_seg, slope)
+        ctx, lse = attend_forward(query, *kv_all, q_pos, segment_ids, key_seg, slope)
         ctx_flat = ctx.reshape(seqs, rows, cols)
         part = jnp.einsum("slc,oc->slo", ctx_flat, w_o, preferred_element_type=jnp.float32)
         mid = state + sum_mp(part) + vec[4]
@@ -529,7 +575,8 @@
     grad = grad_out.astype(jnp.float32)
     gain_rows = [None] * layers
     bias_rows = [None] * layers
-    matrix_grads = [None] * layers
+    finished = [None] * layers
+    pending = []
     for layer in reversed(range(layers)):
         kept_weights, saved = saves[layer]
         (
@@ -562,14 +609,19 @@
             up_gradient_half_precision,
             preferred_element_type=jnp.float32,
         )
-        da2 = sum_mp(
-            jnp.einsum(
-                "cju,xu->cjx",
-                up_gradient_half_precision,
-                up_weight,
-                preferred_element_type=jnp.float32,
-            )
-        )
+        da2 = jnp.einsum(
+            "cju,xu->cjx",
+            up_gradient_half_precision,
+            up_weight,
+            preferred_element_type=jnp.float32,
+        )
+        late = chip_riders(pending)
+        da2, sums = ride_mp(
+            da2, core_riders([up_weight_gradient, grad_wd]) + late, 6 if late else 7
+        )
+        unit_halves = sums[:2]
+        if late:
+            finished[layer + 1] += sums[2:]
         normed2, inverse2 = norm_parts(mid)
         grad_g2 = jnp.sum(da2 * normed2, (0, 1))
         grad_b2 = jnp.sum(da2, (0, 1))
@@ -583,14 +635,14 @@
         query = qkv_bf[:, :, 0].reshape(seqs, rows, heads, HEAD)
         ctx_heads = ctx_flat.reshape(seqs, rows, heads, HEAD)
         dctx_heads = dctx.reshape(seqs, rows, heads, HEAD)
-        grad_q, grad_kv_terms = attend_backward(
-            query, kv_all, q_pos, segment_ids, key_seg, slope, ctx_heads, lse, dctx_heads
-        )
-        kv_terms = jnp.transpose(
-            grad_kv_terms.astype(jnp.bfloat16).reshape(seqs, ctx_count, rows, 2 * cols),
-            (1, 0, 2, 3),
-        )
-        grad_kv = trade([kv_terms], "ctx", 4)[0].reshape(seqs, rows, 2, cols)
+        grad_q, *grad_kv_terms = attend_backward(
+            query, *kv_all, q_pos, segment_ids, key_seg, slope, ctx_heads, lse, dctx_heads
+        )
+        kv_terms = [
+            item.astype(jnp.bfloat16).reshape(seqs, ctx_count, rows, cols)
+            for item in grad_kv_terms
+        ]
+        grad_kv = jnp.stack(trade(kv_terms, "ctx", 4, 1), 2)
         grad_qf = grad_q.reshape(seqs, rows, cols)
         grad_bq = jnp.sum(grad_qf, (0, 1))
         value_bias_gradient = jnp.sum(grad_kv[:, :, 1], (0, 1))
@@ -603,14 +655,20 @@
             packed_projection_gradient,
             preferred_element_type=jnp.float32,
         )
-        da1 = sum_mp(
-            jnp.einsum(
-                "aewu,vwu->aev",
-                packed_projection_gradient,
-                query_weight,
-                preferred_element_type=jnp.float32,
-            )
-        )
+        da1 = jnp.einsum(
+            "aewu,vwu->aev",
+            packed_projection_gradient,
+            query_weight,
+            preferred_element_type=jnp.float32,
+        )
+        da1, sums = ride_mp(
+            da1,
+            core_riders([query_weight_gradient.reshape(width, 3 * cols), grad_wo])
+            + chip_riders(unit_halves),
+            8,
+        )
+        pending = sums[:2]
+        finished[layer] = sums[2:]
         normed1, inverse1 = norm_parts(x_in)
         grad_g1 = jnp.sum(da1 * normed1, (0, 1))
         grad_b1 = jnp.sum(da1, (0, 1))
@@ -628,22 +686,6 @@
         )
         unit_rows = place(grad_bu, mp_index * ff_cols, full_ff).reshape(full_ff // width, width)
         bias_rows[layer] = jnp.concatenate([head_rows, unit_rows], 0)
-        rounded = [
-            item.astype(jnp.bfloat16)
-            for item in (
-                query_weight_gradient.reshape(width, 3 * cols),
-                grad_wo,
-                up_weight_gradient,
-                grad_wd,
-            )
-        ]
-        if layer:
-            matrix_grads[layer] = [
-                lax.psum_scatter(
-                    item, ("batch", "ctx"), scatter_dimension=0, tiled=True
-                ).astype(jnp.float32)
-                for item in rounded
-            ]
     row_count = layers_rows + bias_count
     terms = jnp.concatenate(
         [
@@ -655,13 +697,15 @@
     terms = jnp.transpose(terms, (2, 0, 1, 3)).reshape(mp_count, row_count, owners * part)
     (terms,) = trade([terms], "mp", 5)
     terms = jnp.transpose(terms.reshape(row_count, owners, part), (1, 0, 2))
-    *matrix_grads[0], terms = scatter_all(rounded + [terms.reshape(owners * row_count, part)], 6)
+    (terms,) = trade([terms.reshape(owners // 2, 2, row_count, part)], "core", 9, 1)
+    *tail, terms = trade([item.astype(jnp.bfloat16) for item in pending] + [terms], "chip", 10)
+    finished[0] += tail
     grad_gains = terms[:layers_rows].reshape(gains.shape)
     grad_biases = terms[layers_rows:].reshape(biases.shape)
-    grad_qkv = jnp.stack([item[0] for item in matrix_grads]).reshape(w_qkv.shape)
-    grad_attn_out = jnp.stack([item[1] for item in matrix_grads])
-    grad_up = jnp.stack([item[2] for item in matrix_grads])
-    grad_down = jnp.stack([item[3] for item in matrix_grads])
+    grad_qkv = jnp.stack([item[2] for item in finished]).reshape(w_qkv.shape)
+    grad_attn_out = jnp.stack([item[3] for item in finished])
+    grad_up = jnp.stack([item[0] for item in finished])
+    grad_down = jnp.stack([item[1] for item in finished])
     return (
         output,
         grad.astype(jnp.bfloat16),

time: 732 us -> 631 us (0.86)
  Pallas kernels: 400 us -> 371 us
  local copies, waits for them, and re-layouts: 120 us -> 93.1 us
  other arithmetic: 87.3 us -> 67.2 us
  waiting for transfers between devices: 15.5 us -> 0.09 us
    pallas_call x16, Pallas kernels: 354 us -> 326 us  [the longest x8 236 us: total_mp(): pl.pallas_call(kernel, out_shape=[jax.ShapeDtypeStruct((rows, width), jnp...]
    convert_element_type x17 -> x6, local copies, waits for them, and re-layouts: 42.4 us -> 22.7 us  [core_riders(): a.astype(jnp.bfloat16).reshape(owners // 2, 2, width // owners, a.shape[1])]
    another operation x12 -> x6, local copies, waits for them, and re-layouts: 17.5 us -> 0.02 us  [the longest x4 14.2 us: work(): jnp.stack([grad_k, grad_v], 2).reshape(seqs, block, 2, heads * width)]
    reduce_scatter x3 -> x0, waiting for transfers between devices: 15.4 us -> none  [per_device(): lax.psum_scatter(item, ('batch', 'ctx'), scatter_dimension=0, tiled=True)]
    another operation x12 -> x8, other arithmetic: 20.3 us -> 5.49 us  [the longest x2 8.53 us: work(): jnp.stack([grad_k, grad_v], 2).reshape(seqs, block, 2, heads * width)]
    unnamed x265 -> x256, local copies, waits for them, and re-layouts: 17.4 us -> 17.6 us
  transfers between devices with their start and end apart: 7 -> 3, of which waited for: 1 -> 0; matrix products, arithmetic and copies ran while one was open for 21% -> 10% of each run, Pallas kernels for 36% -> 28%
where the time goes in v2:
time: 631 us; the launch traced here: 621 us
  Pallas kernels  371 us (59%)
  local copies, waits for them, and re-layouts  93.1 us (15%)
  other arithmetic  67.2 us (11%)
  matrix products  64 us (10%)
  between operations  16.2 us (3%)
  blocking collectives  9.8 us (2%)
    pallas_call x8, Pallas kernels, total_mp(): pl.pallas_call(kernel, out_shape=[jax.ShapeDtypeStruct((rows, width), jnp...  236 us
    pallas_call x5, Pallas kernels, trade(): pl.pallas_call(kernel, out_shape=[jax.ShapeDtypeStruct((count - 1,) + cut...  49.6 us
    pallas_call x1, Pallas kernels, spread_all(): pl.pallas_call(kernel, out_shape=[jax.ShapeDtypeStruct((total,) + a.shape...  45 us
    pallas_call x3, Pallas kernels, spread(): pl.pallas_call(kernel, out_shape=[jax.ShapeDtypeStruct(a.shape[:dim] + (c...  39.9 us
    convert_element_type x6, local copies, waits for them, and re-layouts, core_riders(): a.astype(jnp.bfloat16).reshape(owners // 2, 2, width // owners, a.shape[1])  22.7 us
    unnamed x256, local copies, waits for them, and re-layouts  17.6 us
  transfers between devices with their start and end apart: 3, of which 0 were waited for; matrix products, arithmetic and copies ran while one was open for 10% of the time, Pallas kernels for 28%

profile of v2, /device:TPU:0, one launch (start us, length us, event | category | flops | bytes accessed | tf_op | source)
XLA Modules:
  0.0 621.0 jit_solution(17298064051499700917)
XLA Ops:
  7.2 1.8 fusion.181
  11.1 7.7 %spread_mp.1 = bf16[4,24,32]{2,1,0:T(8,128)(2,1)} custom-call(bf16[24,32]{1,0:T(8,128)(2,1)} %pad_maximum_fusion.10.refs_0_), custom_call_target="tpu_custom_call" | custom-call | tf_op jit(solution)/shard_map/spread_mp/pallas_call | solution.py:205
  24.0 45.0 %spread_all.1 = (bf16[8,128,768]{2,1,0:T(8,128)(2,1)}, bf16[8,128,256]{2,1,0:T(8,128)(2,1)}, bf16[8,128,1024]{2,1,0:T(8,128)(2,1)}, bf16[8,128,1024]{2,1,0:T(8,1...) custom-call(bf16[128,768]{1,0:T(8,128)(2,1)} %copy.73.refs_0_, bf16[128,256]{1,0:T(8,128)(2,1)} %slice_bitcast_fusion.6.refs_1_, ...), custom_call_target="tpu_custom_call" | custom-call | tf_op jit(solution)/shard_map/spread_all/pallas_call | solution.py:270
  74.2 2.0 copy.76
  76.2 2.6 reshape.950
  86.3 18.9 %spread_ctx.2 = (bf16[2,4,128,256]{3,2,1,0:T(8,128)(2,1)}, bf16[2,4,128,256]{3,2,1,0:T(8,128)(2,1)}) custom-call(bf16[2,128,256]{2,1,0:T(8,128)(2,1)} %get-tuple-element.137.refs_0_, bf16[2,128,256]{2,1,0:T(8,128)(2,1)} %get-tuple-element.136.refs_1_), custom_call_target="tpu_custom_call" | custom-call | tf_op jit(solution)/shard_map/spread_ctx/pallas_call | solution.py:205
  112.1 27.0 %total_mp.8 = bf16[256,1024]{1,0:T(8,128)(2,1)} custom-call(bf16[256,1024]{1,0:T(8,128)(2,1)} %convolution_convert_fusion.3.x_ref), custom_call_target="tpu_custom_call" | custom-call | tf_op jit(solution)/shard_map/total_mp/pallas_call | solution.py:160
  142.6 3.7 multiply_convert_fusion.3
  146.4 1.6 convolution_convert_fusion.5.x_ref
  148.0 30.6 %total_mp.9 = bf16[256,1024]{1,0:T(8,128)(2,1)} custom-call(bf16[256,1024]{1,0:T(8,128)(2,1)} %convolution_convert_fusion.5.x_ref), custom_call_target="tpu_custom_call" | custom-call | tf_op jit(solution)/shard_map/total_mp/pallas_call | solution.py:160
  184.0 9.8 %all-gather.1 = bf16[1,1024,256]{2,1,0:T(8,128)(2,1)S(1)} all-gather(bf16[1,128,256]{2,1,0:T(8,128)(2,1)S(1)} %copy-done.56), channel_id=3, replica_groups=mesh['batch'=2,'ctx'=4,'mp'=4] {'batch','ctx'}, dimensions={1}, use_global_device_ids=true | all-gather | bytes 589824 | tf_op jit(solution)/shard_map/all_gather | solution.py:568
  194.6 2.0 fusion.58
  197.6 13.3 %spread_ctx.3 = (bf16[2,4,128,256]{3,2,1,0:T(8,128)(2,1)}, bf16[2,4,128,256]{3,2,1,0:T(8,128)(2,1)}) custom-call(bf16[2,128,256]{2,1,0:T(8,128)(2,1)} %get-tuple-element.130.refs_0_, bf16[2,128,256]{2,1,0:T(8,128)(2,1)} %get-tuple-element.129.refs_1_), custom_call_target="tpu_custom_call" | custom-call | tf_op jit(solution)/shard_map/spread_ctx/pallas_call | solution.py:205
  216.2 2.4 fusion.22
  221.5 28.4 %total_mp.10 = bf16[256,1024]{1,0:T(8,128)(2,1)} custom-call(bf16[256,1024]{1,0:T(8,128)(2,1)} %convolution_convert_fusion.2.x_ref), custom_call_target="tpu_custom_call" | custom-call | tf_op jit(solution)/shard_map/total_mp/pallas_call | solution.py:160
  251.4 3.4 fusion.27
  254.8 3.5 fusion.42
  258.4 30.2 %total_mp.11 = bf16[256,1024]{1,0:T(8,128)(2,1)} custom-call(bf16[256,1024]{1,0:T(8,128)(2,1)} %bitcast.582), custom_call_target="tpu_custom_call" | custom-call | tf_op jit(solution)/shard_map/total_mp/pallas_call | solution.py:160
  288.6 3.8 bitcast_convert_fusion.2
  292.4 1.8 fusion.187
  294.2 2.2 bitcast_convert_fusion.3
  296.4 1.5 fusion.39
  298.0 29.1 %total_mp.12 = (bf16[256,1024]{1,0:T(8,128)(2,1)}, bf16[1,4,128,1024]{3,2,1,0:T(8,128)(2,1)}, bf16[1,4,128,1024]{3,2,1,0:T(8,128)(2,1)}) custom-call(bf16[256,1024]{1,0:T(8,128)(2,1)} %bitcast.579, bf16[4,2,128,1024]{3,2,1,0:T(8,128)(2,1)} %bitcast.546, bf16[4,2,128,1024]{3,2,1,0:T(8,128)(2,1)} %bitcast.554), custom_call_target="tpu_custom_call" | custom-call | tf_op jit(solution)/shard_map/total_mp/pallas_call | solution.py:160
  327.1 2.0 convert_reduce_fusion.5
  329.1 2.2 multiply_reduce_fusion
  331.4 2.0 fusion.174
  336.6 3.4 fusion.69
  348.4 13.5 %trade_ctx.2 = (bf16[3,2,128,256]{3,2,1,0:T(8,128)(2,1)}, bf16[3,2,128,256]{3,2,1,0:T(8,128)(2,1)}) custom-call(bf16[2,4,128,256]{3,2,1,0:T(8,128)(2,1)} %copy.96.refs_0_, bf16[2,4,128,256]{3,2,1,0:T(8,128)(2,1)} %copy.97.refs_1_), custom_call_target="tpu_custom_call" | custom-call | tf_op jit(solution)/shard_map/trade_ctx/pallas_call | solution.py:304
  361.9 1.7 fusion.133
  365.7 2.9 bitcast_convert_fusion.5
  368.6 2.6 copy.102
  371.2 3.8 convert_element_type.963
  374.9 4.9 copy.107.refs_0_
  379.9 4.3 constant_dynamic-slice_fusion.3
  389.0 4.8 copy.161
  393.9 3.0 fusion.36
  396.8 30.8 %total_mp.13 = (bf16[256,1024]{1,0:T(8,128)(2,1)}, bf16[1,4,128,768]{3,2,1,0:T(8,128)(2,1)}, bf16[1,4,128,256]{3,2,1,0:T(8,128)(2,1)}, bf16[3,128,1024]{2,1,0:T(8,128)(2,1)}, bf16[3,128,1024]{2,1,0:T(8,128)(2,1)}) custom-call(bf16[256,1024]{1,0:T(8,128)(2,1)} %bitcast.578, bf16[4,2,128,768]{3,2,1,0:T(8,128)(2,1)} %copy.107.refs_0_, ...), custom_call_target="tpu_custom_call" | custom-call | tf_op jit(solution)/shard_map/total_mp/pallas_call | solution.py:160
  427.6 1.9 fusion.122.refs_3_
  430.8 1.6 multiply_reduce_fusion.1
  433.5 2.1 bitcast_convert_fusion
  436.9 2.3 bitcast_convert_fusion.1
  441.1 1.5 convolution_convert_fusion.4.x_ref
  442.6 28.3 %total_mp.14 = (bf16[256,1024]{1,0:T(8,128)(2,1)}, bf16[1,4,128,1024]{3,2,1,0:T(8,128)(2,1)}, bf16[1,4,128,1024]{3,2,1,0:T(8,128)(2,1)}, bf16[3,128,768]{2,1,0:T(8,128)(2,1)}, bf16[3,128,256]{2,1,0:T(8,128)(2,1)}) custom-call(bf16[256,1024]{1,0:T(8,128)(2,1)} %convolution_convert_fusion.4.x_ref, bf16[4,2,128,1024]{3,2,1,0:T(8,128)(2,1)} %bitcast.556, ...), custom_call_target="tpu_custom_call" | custom-call | tf_op jit(solution)/shard_map/total_mp/pallas_call | solution.py:160
  472.4 1.9 multiply_reduce_fusion.2
  475.9 3.4 fusion.70
  484.5 12.6 %trade_ctx.3 = (bf16[3,2,128,256]{3,2,1,0:T(8,128)(2,1)}, bf16[3,2,128,256]{3,2,1,0:T(8,128)(2,1)}) custom-call(bf16[2,4,128,256]{3,2,1,0:T(8,128)(2,1)} %copy.114.refs_0_, bf16[2,4,128,256]{3,2,1,0:T(8,128)(2,1)} %copy.115.refs_1_), custom_call_target="tpu_custom_call" | custom-call | tf_op jit(solution)/shard_map/trade_ctx/pallas_call | solution.py:304
  500.1 1.9 bitcast_convert_fusion.4
  502.0 2.6 copy.120
  504.7 3.8 convert_element_type.1024
  508.4 4.3 constant_dynamic-slice_fusion
  512.7 5.0 copy.125.refs_0_
  518.3 3.1 fusion.refs_3_
  522.9 2.8 fusion.35.x_ref
  526.8 3.4 copy.167
  530.3 31.8 %total_mp.15 = (bf16[256,1024]{1,0:T(8,128)(2,1)}, bf16[1,4,128,768]{3,2,1,0:T(8,128)(2,1)}, bf16[1,4,128,256]{3,2,1,0:T(8,128)(2,1)}, bf16[3,128,1024]{2,1,0:T(8,128)(2,1)}, bf16[3,128,1024]{2,1,0:T(8,128)(2,1)}) custom-call(bf16[256,1024]{1,0:T(8,128)(2,1)} %fusion.35.x_ref, bf16[4,2,128,768]{3,2,1,0:T(8,128)(2,1)} %copy.125.refs_0_, ...), custom_call_target="tpu_custom_call" | custom-call | tf_op jit(solution)/shard_map/total_mp/pallas_call | solution.py:160
  562.1 1.7 fusion.121.refs_1_
  563.8 1.9 convert_reduce_fusion.2
  565.8 2.2 fusion.84
  570.0 6.7 %trade_mp.1 = f32[3,24,256]{2,1,0:T(8,128)} custom-call(f32[4,24,256]{2,1,0:T(8,128)} %reshape.976.refs_0_), custom_call_target="tpu_custom_call" | custom-call | tf_op jit(solution)/shard_map/trade_mp/pallas_call | solution.py:304
  578.2 1.6 trade_core.1
  581.3 2.2 fusion.14.refs_0_
  583.5 15.2 %trade_chip.1 = (bf16[3,128,768]{2,1,0:T(8,128)(2,1)}, bf16[3,128,256]{2,1,0:T(8,128)(2,1)}, f32[3,24,32]{2,1,0:T(8,128)}) custom-call(bf16[4,128,768]{2,1,0:T(8,128)(2,1)} %fusion.14.refs_0_, bf16[4,128,256]{2,1,0:T(8,128)(2,1)} %fusion.121.refs_1_, f32[4,24,32]{2,1,0:T(8,128)} %bitcast_add_fusion.refs_2_), custom_call_target="tpu_custom_call" | custom-call | tf_op jit(solution)/shard_map/trade_chip/pallas_call | solution.py:304
  606.4 1.8 convert_add_fusion.13
  608.3 1.7 convert_add_fusion.14
  (459 shorter events, 101.1 us)
Async XLA Ops:
  7.2 15.4 %copy-start.26 = (bf16[2,128,1024]{2,1,0:T(8,128)(2,1)S(1)}, bf16[2,128,1024]{2,1,0:T(8,128)(2,1)}, u32[]{:S(2)}) copy-start(bf16[2,128,1024]{2,1,0:T(8,128)(2,1)} %param.15) | copy-start | bytes 1572868
  7.2 16.1 %copy-start.27 = (bf16[2,128,1024]{2,1,0:T(8,128)(2,1)S(1)}, bf16[2,128,1024]{2,1,0:T(8,128)(2,1)}, u32[]{:S(2)}) copy-start(bf16[2,128,1024]{2,1,0:T(8,128)(2,1)} %param.16) | copy-start | bytes 1572868
  7.2 186.9 %all-gather.8.cloned.1.call-start = ((), (), s32[]{:S(2)}) async-start(), calls=%async_computation | async-start | bytes 1769472 | tf_op jit(solution)/shard_map/all_gather | solution.py:567
  9.1 242.4 %all-gather.10.cloned.1.call-start = ((), (), s32[]{:S(2)}) async-start(), calls=%async_computation.1 | async-start | bytes 2359296 | tf_op jit(solution)/shard_map/all_gather | solution.py:569
  23.3 48.4 %copy-start.57 = (bf16[4,24,32]{2,1,0:T(8,128)(2,1)S(1)}, bf16[4,24,32]{2,1,0:T(8,128)(2,1)}, u32[]{:S(2)}) copy-start(bf16[4,24,32]{2,1,0:T(8,128)(2,1)} %constant_dynamic-update-slice_fusion.6) | copy-start | bytes 18436
  69.1 3.9 copy-start
  69.9 4.3 copy-start.25
  69.9 184.9 %all-gather.12.cloned.1.call-start = ((), (), s32[]{:S(2)}) async-start(), calls=%async_computation.2 | async-start | bytes 2359296 | tf_op jit(solution)/shard_map/all_gather | solution.py:570
  73.2 11.5 %copy-start.74 = (f32[2,128]{1,0:T(2,128)}, f32[2,128]{1,0:T(2,128)S(1)}, u32[]{:S(2)}) copy-start(f32[2,128]{1,0:T(2,128)S(1)} %broadcast_multiply_fusion.8) | copy-start | bytes 3076
  73.5 11.2 %copy-start.88 = (f32[2,128]{1,0:T(2,128)}, f32[2,128]{1,0:T(2,128)S(1)}, u32[]{:S(2)}) copy-start(f32[2,128]{1,0:T(2,128)S(1)} %add_rsqrt_fusion.3) | copy-start | bytes 3076
  78.8 6.6 %copy-start.11 = (bf16[1024,3,256]{0,2,1:T(8,128)(2,1)}, bf16[1024,3,256]{0,2,1:T(8,128)(2,1)S(1)}, u32[]{:S(2)}) copy-start(bf16[1024,3,256]{0,2,1:T(8,128)(2,1)S(1)} %reshape.950) | copy-start | bytes 4718596
  79.6 31.4 %copy-start.20 = (bf16[8,128,256]{2,1,0:T(8,128)(2,1)}, bf16[8,128,256]{2,1,0:T(8,128)(2,1)S(1)}, u32[]{:S(2)}) copy-start(bf16[8,128,256]{2,1,0:T(8,128)(2,1)S(1)} %get-tuple-element.158) | copy-start | bytes 1572868
  86.2 22.2 %copy-start.48 = (bf16[2,128,1,256]{1,3,0,2:T(8,128)(2,1)}, bf16[2,128,1,256]{1,3,0,2:T(8,128)(2,1)S(1)}, u32[]{:S(2)}) copy-start(bf16[2,128,1,256]{1,3,0,2:T(8,128)(2,1)S(1)} %copy.81) | copy-start | bytes 393220
  111.0 31.6 %copy-start.101 = (f32[1024]{0:T(1024)S(1)}, f32[1024]{0:T(1024)}, u32[]{:S(2)}) copy-start(f32[1024]{0:T(1024)} %reshape.985) | copy-start | bytes 12292
  140.5 5.8 copy-start.84
  141.9 4.5 copy-start.92
  142.6 3.8 copy-start.114
  146.4 32.2 %copy-start.40 = (bf16[2,128,1024]{2,1,0:T(8,128)(2,1)}, bf16[2,128,1024]{2,1,0:T(8,128)(2,1)S(1)}, u32[]{:S(2)}) copy-start(bf16[2,128,1024]{2,1,0:T(8,128)(2,1)S(1)} %get-tuple-element.167) | copy-start | bytes 1572868
  146.4 32.2 %copy-start.78 = (f32[1024]{0:T(1024)S(1)}, f32[1024]{0:T(1024)}, u32[]{:S(2)}) copy-start(f32[1024]{0:T(1024)} %reshape.987) | copy-start | bytes 12292
  148.0 33.8 %copy-start.71 = (f32[1,8,4,32]{3,2,1,0:T(4,128)S(1)}, f32[1,8,4,32]{3,2,1,0:T(4,128)}, u32[]{:S(2)}) copy-start(f32[1,8,4,32]{3,2,1,0:T(4,128)} %get-tuple-element.142) | copy-start | bytes 12292
  148.0 34.5 %copy-start.70 = (f32[1,8,4,32]{3,2,1,0:T(4,128)S(1)}, f32[1,8,4,32]{3,2,1,0:T(4,128)}, u32[]{:S(2)}) copy-start(f32[1,8,4,32]{3,2,1,0:T(4,128)} %get-tuple-element.143) | copy-start | bytes 12292
  148.0 35.2 %copy-start.69 = (f32[1,8,4,32]{3,2,1,0:T(4,128)S(1)}, f32[1,8,4,32]{3,2,1,0:T(4,128)}, u32[]{:S(2)}) copy-start(f32[1,8,4,32]{3,2,1,0:T(4,128)} %get-tuple-element.147) | copy-start | bytes 12292
  148.0 35.2 %copy-start.68 = (f32[1,8,4,32]{3,2,1,0:T(4,128)S(1)}, f32[1,8,4,32]{3,2,1,0:T(4,128)}, u32[]{:S(2)}) copy-start(f32[1,8,4,32]{3,2,1,0:T(4,128)} %get-tuple-element.144) | copy-start | bytes 12292
  178.6 5.5 copy-start.56
  178.6 16.1 %copy-start.72 = (f32[1,1,1024]{2,1,0:T(1,128)S(1)}, f32[1,1,1024]{2,1,0:T(1,128)}, u32[]{:S(2)}) copy-start(f32[1,1,1024]{2,1,0:T(1,128)} %get-tuple-element.160) | copy-start | bytes 12292
  178.6 16.1 %copy-start.104 = (f32[3,256]{1,0:T(4,128)S(1)}, f32[3,256]{1,0:T(4,128)}, u32[]{:S(2)}) copy-start(f32[3,256]{1,0:T(4,128)} %get-tuple-element.163) | copy-start | bytes 9220
  183.2 10.9 %copy-start.103 = (f32[1024]{0:T(1024)}, f32[1024]{0:T(1024)S(1)}, u32[]{:S(2)}) copy-start(f32[1024]{0:T(1024)S(1)} %reshape.989) | copy-start | bytes 12292
  193.8 26.5 %copy-start.13 = (bf16[1,1024,256]{2,1,0:T(8,128)(2,1)}, bf16[1,1024,256]{2,1,0:T(8,128)(2,1)S(1)}, u32[]{:S(2)}) copy-start(bf16[1,1024,256]{2,1,0:T(8,128)(2,1)S(1)} %all-gather.1) | copy-start | bytes 1572868
  197.5 18.7 %copy-start.50 = (bf16[2,128,1,256]{1,3,0,2:T(8,128)(2,1)}, bf16[2,128,1,256]{1,3,0,2:T(8,128)(2,1)S(1)}, u32[]{:S(2)}) copy-start(bf16[2,128,1,256]{1,3,0,2:T(8,128)(2,1)S(1)} %copy.88) | copy-start | bytes 393220
  211.5 4.7 copy-start.65
  220.1 29.7 %copy-start.79 = (f32[1024]{0:T(1024)S(1)}, f32[1024]{0:T(1024)}, u32[]{:S(2)}) copy-start(f32[1024]{0:T(1024)} %reshape.991) | copy-start | bytes 12292
  288.6 3.8 copy-start.38
  288.6 3.8 copy-start.113
  288.6 3.8 copy-start.121
  327.1 4.3 copy-start.7
  327.1 4.3 copy-start.18
  327.1 4.3 copy-start.39
  327.1 4.3 copy-start.76
  347.3 18.4 %copy-start.73 = (f32[1,1,1024]{2,1,0:T(1,128)S(1)}, f32[1,1,1024]{2,1,0:T(1,128)}, u32[]{:S(2)}) copy-start(f32[1,1,1024]{2,1,0:T(1,128)} %get-tuple-element.160) | copy-start | bytes 12292
  364.7 3.9 copy-start.61
  365.7 5.5 copy-start.63
  379.9 4.4 copy-start.12
  379.9 4.4 copy-start.34
  387.9 6.0 copy-start.62
  396.8 34.0 %copy-start.87 = (f32[2,128]{1,0:T(2,128)S(1)}, f32[2,128]{1,0:T(2,128)}, u32[]{:S(2)}) copy-start(f32[2,128]{1,0:T(2,128)} %copy-done.86) | copy-start | bytes 3076
  396.8 34.0 %copy-start.95 = (f32[2,128]{1,0:T(2,128)S(1)}, f32[2,128]{1,0:T(2,128)}, u32[]{:S(2)}) copy-start(f32[2,128]{1,0:T(2,128)} %copy-done.94) | copy-start | bytes 3076
  427.6 4.9 copy-start.9
  432.9 4.0 copy-start.5
  484.5 15.6 %copy-start.75 = (f32[2,128]{1,0:T(2,128)S(1)}, f32[2,128]{1,0:T(2,128)}, u32[]{:S(2)}) copy-start(f32[2,128]{1,0:T(2,128)} %copy-done.74) | copy-start | bytes 3076
  484.5 15.6 %copy-start.89 = (f32[2,128]{1,0:T(2,128)S(1)}, f32[2,128]{1,0:T(2,128)}, u32[]{:S(2)}) copy-start(f32[2,128]{1,0:T(2,128)} %copy-done.88) | copy-start | bytes 3076
  484.5 15.6 %copy-start.100 = (f32[1024]{0:T(1024)S(1)}, f32[1024]{0:T(1024)}, u32[]{:S(2)}) copy-start(f32[1024]{0:T(1024)} %copy-done.99) | copy-start | bytes 12292
  512.7 5.0 copy-start.106
  512.7 5.3 copy-start.96
  517.7 3.8 copy-start.32
  530.3 31.8 %copy-start.16 = (bf16[1024,256]{1,0:T(8,128)(2,1)S(1)}, bf16[1024,256]{1,0:T(8,128)(2,1)}, u32[]{:S(2)}) copy-start(bf16[1024,256]{1,0:T(8,128)(2,1)} %fusion.48) | copy-start | bytes 1572868
  562.1 5.9 copy-start.83
  562.1 6.1 copy-start.81
  562.1 6.1 copy-start.82
  562.1 6.2 copy-start.97
  562.1 6.2 copy-start.80
  577.5 22.6 %copy-start.58 = (bf16[3,128,256]{2,1,0:T(8,128)(2,1)S(1)}, bf16[3,128,256]{2,1,0:T(8,128)(2,1)}, u32[]{:S(2)}) copy-start(bf16[3,128,256]{2,1,0:T(8,128)(2,1)} %get-tuple-element.73) | copy-start | bytes 589828
  578.2 22.8 %copy-start.37 = (bf16[3,128,768]{2,1,0:T(8,128)(2,1)S(1)}, bf16[3,128,768]{2,1,0:T(8,128)(2,1)}, u32[]{:S(2)}) copy-start(bf16[3,128,768]{2,1,0:T(8,128)(2,1)} %get-tuple-element.71) | copy-start | bytes 1769476
  583.5 18.7 %copy-start.109 = (f32[2,128]{1,0:T(2,128)S(1)}, f32[2,128]{1,0:T(2,128)}, u32[]{:S(2)}) copy-start(f32[2,128]{1,0:T(2,128)} %get-tuple-element.101) | copy-start | bytes 3076
  583.5 18.7 %copy-start.98 = (f32[256]{0:T(256)S(1)}, f32[256]{0:T(256)}, u32[]{:S(2)}) copy-start(f32[256]{0:T(256)} %get-tuple-element.105) | copy-start | bytes 3076
  (62 other events, 134.3 us)
Sparse Core Ops, SparseCore 0:
  10.5 34.1 all-gather.7
  70.1 33.0 all-gather.9
  105.0 27.7 all-gather.11
